TPU v7x, 32 devices: a whole 2x2x4 slice. The times are simulated.
32 devices in a mesh: grp: 2 (over x), wide: 16 (over z, y, core).
Axes of the slice: x: 2, y: 2, z: 4, core: 2. Of those that a mesh axis runs over, the one named last changes fastest.
Arguments:
- homolog_stack_state: bfloat16 [256, 128, 256], P(('grp', 'wide')), parts along dimension 0, may hold values from -6 to 6
- present_flags: int32 [256, 128], P('grp'), parts along dimension 0, may hold values from 0 to 1, as said below
- chain_ordinal_labels: int32 [256], P('grp'), parts along dimension 0, may hold values from 0 to 383, as said below
- pairwise_repr: bfloat16 [256, 128, 128], P(('grp', 'wide')), parts along dimension 0, may hold values from -6 to 6
- heeding_normalizer_gains: float32 [256], replicated, may hold values from 0.1 to 1.9
- retrieval_weights_qkv: bfloat16 [256, 768], replicated, may hold values from -2.7308912 to 2.7308912
- logistic_weights: bfloat16 [256, 256], replicated, may hold values from -0.375 to 0.375
- logistic_intercept: float32 [256], replicated, may hold values from -4 to 4
- emitted_weights: bfloat16 [256, 256], replicated, may hold values from -0.375 to 0.375
- dyadic_normalizer_gains: float32 [256], replicated, may hold values from 0.1 to 1.9
- former_operand_weights: bfloat16 [256, 32], replicated, may hold values from -0.375 to 0.375
- latter_operand_weights: bfloat16 [256, 32], replicated, may hold values from -0.375 to 0.375
- flattened_outer_projection: bfloat16 [1024, 128], replicated, may hold values from -0.75 to 0.75
- clipped_separation_embedding: bfloat16 [65, 128], replicated, may hold values from -5 to 5
Outputs:
- homolog_changed: bfloat16 [256, 128, 256], P(('grp', 'wide')), parts along dimension 0
- couple_state_changed: bfloat16 [256, 128, 128], P(('grp', 'wide')), parts along dimension 0
There are 2 independent parts, one for each index of `grp`. A program takes and returns all parts, laid end to end along the dimension named above; an argument that names none is the same for every part. Nothing has to cross between parts.
Inputs may be any that keep to these rules, and one draw needn't show every extreme that they name: `present_flags`: every entry of the first sequence is 1. `chain_ordinal_labels`: rises from token to token by 1 to 3.
All inputs are finite; a program needn't handle non-finite values.
Results may differ from a plain program's by a relative error of at most 0.0094.
The roundings to bfloat16 on the way count: a program that leaves them out, or rounds other values in their place, can miss the bound.
Values may be sent and summed in bfloat16 or wider, within the bound.
No kernel may reach another device: no remote copies, remote signals or barrier semaphores. Data moves between devices by JAX's collectives and lax.ppermute only.
A program may use at most 128 MiB of HBM per device.

v0:
```python
import functools
import math

import jax
import jax.numpy as jnp
from jax import lax
from jax.experimental import pallas as pl
from jax.experimental.pallas import tpu as pltpu
from jax.sharding import PartitionSpec as P


RELPOS_CLIP = 32
HEAD_SIZE = 32
EPSILON = 1e-05
LANES = 128
F32 = jnp.float32
BF16 = jnp.bfloat16


NT = (((1,), (1,)), ((), ()))
TN = (((0,), (0,)), ((), ()))


def standardize(values, gain_row):
    mean = jnp.mean(values, axis=-1, keepdims=True)
    centered = values - mean
    variance = jnp.mean(centered * centered, axis=-1, keepdims=True)
    return centered * lax.rsqrt(variance + EPSILON) * gain_row


def put_rows(ref, rows, values):
    for part in range(ref.shape[0]):
        ref[part, rows, :] = values[:, part * LANES : (part + 1) * LANES]


def take_rows(ref, rows):
    return jnp.concatenate([ref[part, rows, :] for part in range(ref.shape[0])], axis=1)


def attention_kernel(
    tokens,
    x_ref,
    bias_ref,
    flag_ref,
    gains_ref,
    wqvg_ref,
    wk_ref,
    intercept_ref,
    wo_ref,
    wlr_ref,
    hc_ref,
    left_ref,
    right_ref,
    xf_ref,
    normed_ref,
    hcf_ref,
    rf_ref,
    queries_ref,
    keys_ref,
    values_ref,
    gate_ref,
    gated_ref,
    *group_refs,
):
    logits_refs, weights_refs = group_refs[::2], group_refs[1::2]
    rows, channels = x_ref.shape
    seqs = rows // tokens
    breadth = wlr_ref.shape[0] // 2
    group_heads = LANES // HEAD_SIZE
    scale = math.log2(math.e) / math.sqrt(HEAD_SIZE)

    values = x_ref[...].astype(F32)
    put_rows(xf_ref, slice(None), values)
    put_rows(normed_ref, slice(None), standardize(values, gains_ref[0:1, :]))

    def rows_of(ref, t):
        return take_rows(ref, pl.ds(t, seqs, stride=tokens))

    normed = jnp.concatenate([rows_of(normed_ref, t) for t in range(tokens)], axis=0).astype(BF16)
    qvg = lax.dot_general(wqvg_ref[...], normed, NT, preferred_element_type=F32)
    keys = jnp.dot(normed, wk_ref[...], preferred_element_type=F32).astype(BF16)
    gate = 0.5 * jnp.tanh(0.5 * (qvg[2 * channels :] + intercept_ref[...])) + 0.5
    for t in range(tokens):
        at = slice(t * seqs, (t + 1) * seqs)
        queries_ref[t] = qvg[:channels, at].astype(BF16)
        values_ref[t] = qvg[channels : 2 * channels, at].astype(BF16)
        gate_ref[t] = gate[:, at]
        keys_ref[t] = keys[at]

    groups = channels // LANES

    def score(t, held):
        token_row = lax.broadcasted_iota(jnp.int32, (LANES, seqs), 0) == t
        token_row = jnp.where(token_row, 1.0, 0.0).astype(BF16)
        for g in range(groups):
            keys_g = jnp.concatenate(
                [keys_ref[t, :, g * LANES : (g + 1) * LANES], bias_ref[...]], axis=1
            )
            columns = []
            for h in range(group_heads):
                first = g * LANES + h * HEAD_SIZE
                parts = [queries_ref[t, first : first + HEAD_SIZE], token_row]
                above, below = h * HEAD_SIZE, LANES - (h + 1) * HEAD_SIZE
                if below:
                    parts.insert(1, jnp.zeros((below, seqs), BF16))
                if above:
                    parts.insert(0, jnp.zeros((above, seqs), BF16))
                columns.append(jnp.concatenate(parts, axis=0))
            logits_refs[held][g] = jnp.dot(
                keys_g, jnp.concatenate(columns, axis=1), preferred_element_type=F32
            )

    def weigh(held):
        for g in range(groups):
            for h in range(group_heads):
                head = slice(h * seqs, (h + 1) * seqs)
                logits = logits_refs[held][g, :, head]
                highest = jnp.max(logits, axis=0, keepdims=True)
                powers = jnp.exp2((logits - highest) * scale)
                share = 1.0 / jnp.sum(powers, axis=0, keepdims=True)
                weights_refs[held][g, :, head] = (powers * share).astype(BF16)

    def mix(t, held):
        for g in range(groups):
            for h in range(group_heads):
                head = slice(g * LANES + h * HEAD_SIZE, g * LANES + (h + 1) * HEAD_SIZE)
                mixed = jnp.dot(
                    values_ref[t, head],
                    weights_refs[held][g, :, h * seqs : (h + 1) * seqs],
                    preferred_element_type=F32,
                )
                gated_ref[t, head] = (mixed * gate_ref[t, head]).astype(BF16)

    score(0, 0)
    for t in range(tokens):
        if t > 0:
            mix(t - 1, (t - 1) % 2)
        weigh(t % 2)
        if t + 1 < tokens:
            score(t + 1, (t + 1) % 2)
    mix(tokens - 1, (tokens - 1) % 2)

    for t in range(tokens):
        delta = lax.dot_general(gated_ref[t], wo_ref[...], TN, preferred_element_type=F32)
        changed = (rows_of(xf_ref, t) + delta).astype(BF16).astype(F32)
        put_rows(hcf_ref, pl.ds(t, seqs, stride=tokens), changed)
        normed2 = standardize(changed, gains_ref[1:2, :]).astype(BF16)
        factors = lax.dot_general(wlr_ref[...], normed2, NT, preferred_element_type=F32)
        factors = factors * flag_ref[t]
        left_ref[t] = factors[:breadth].astype(BF16)
        rf_ref[pl.ds(t, breadth, stride=tokens), :] = factors[breadth:]

    hc_ref[...] = take_rows(hcf_ref, slice(None)).astype(BF16)
    right_ref[...] = rf_ref[...].astype(BF16)


def attention(x_rows, bias, flag_rows, gains, wqvg, wk, intercept, wo, wlr, tokens):
    rows, channels = x_rows.shape
    seqs = rows // tokens
    breadth = wlr.shape[0] // 2
    groups, group_heads = channels // LANES, LANES // HEAD_SIZE
    slab = pltpu.VMEM((channels // LANES, rows, LANES), F32)
    vmem = pl.BlockSpec(memory_space=pltpu.VMEM)
    return pl.pallas_call(
        functools.partial(attention_kernel, tokens),
        out_shape=(
            jax.ShapeDtypeStruct((rows, channels), BF16),
            jax.ShapeDtypeStruct((tokens, breadth, seqs), BF16),
            jax.ShapeDtypeStruct((breadth * tokens, seqs), BF16),
        ),
        in_specs=[vmem] * 9,
        out_specs=(vmem, vmem, vmem),
        scratch_shapes=[
            slab,
            slab,
            slab,
            pltpu.VMEM((breadth * tokens, seqs), F32),
            pltpu.VMEM((tokens, channels, seqs), BF16),
            pltpu.VMEM((tokens, seqs, channels), BF16),
            pltpu.VMEM((tokens, channels, seqs), BF16),
            pltpu.VMEM((tokens, channels, seqs), F32),
            pltpu.VMEM((tokens, channels, seqs), BF16),
        ]
        + [
            pltpu.VMEM((groups, seqs, group_heads * seqs), F32),
            pltpu.VMEM((groups, seqs, group_heads * seqs), BF16),
        ]
        * 2,
        compiler_params=pltpu.CompilerParams(vmem_limit_bytes=24 * 2**20),
        cost_estimate=pl.CostEstimate(
            flops=2 * rows * channels * (6 * channels),
            bytes_accessed=4 * rows * channels,
            transcendentals=0,
        ),
        name="attention",
    )(x_rows, bias, flag_rows, gains, wqvg, wk, intercept, wo, wlr)


def pair_kernel(
    stages, per_device, me_ref, left_ref, weight_ref, share_ref, base_ref, *refs
):
    held_refs, (out_ref, right_ref, outer_ref) = refs[:-3], refs[-3:]
    tok_local, breadth, seqs = left_ref.shape
    width = out_ref.shape[1]
    first = pl.program_id(0) * (width // per_device)
    me = me_ref[0]
    (far, far_size), (near, near_size), (core, core_size) = stages

    @pl.when(pl.program_id(0) == 0)
    def _():
        for n in range(near_size):
            for c in range(core_size):
                for f in range(far_size):
                    device = jnp.bitwise_xor(me, f * far + n * near + c * core)
                    right_ref[device] = held_refs[n * core_size + c][f]

    left = left_ref[...].reshape(tok_local * breadth, seqs)
    for e in range(breadth):
        right = jnp.concatenate(
            [
                right_ref[first + d, e * per_device : (e + 1) * per_device, :]
                for d in range(width // per_device)
            ],
            axis=0,
        )
        outer = lax.dot_general(left, right, NT, preferred_element_type=F32).astype(BF16)
        outer_ref[:, e * breadth : (e + 1) * breadth, :] = outer.reshape(tok_local, breadth, width)

    for i in range(tok_local):
        projected = jnp.dot(weight_ref[...], outer_ref[i], preferred_element_type=F32)
        projected = projected * share_ref[i : i + 1, :]
        out_ref[i] = (base_ref[i] + projected.T).astype(BF16)


def pair_update(me, left, right_held, weight_t, share, base, stages):
    tok_local, breadth, seqs = left.shape
    pair_width = weight_t.shape[0]
    block = right_held[0].shape[1:]
    per_device = block[0] // breadth
    columns = base.shape[1]
    width = min(columns, LANES)
    return pl.pallas_call(
        functools.partial(pair_kernel, stages, per_device),
        grid_spec=pltpu.PrefetchScalarGridSpec(
            num_scalar_prefetch=1,
            grid=(columns // width,),
            in_specs=[
                pl.BlockSpec(left.shape, lambda j, me: (0, 0, 0)),
                pl.BlockSpec(weight_t.shape, lambda j, me: (0, 0)),
                pl.BlockSpec((tok_local, width), lambda j, me: (0, j)),
                pl.BlockSpec((tok_local, width, pair_width), lambda j, me: (0, j, 0)),
            ]
            + [pl.BlockSpec(held.shape, lambda j, me: (0, 0, 0)) for held in right_held],
            out_specs=pl.BlockSpec((tok_local, width, pair_width), lambda j, me: (0, j, 0)),
            scratch_shapes=[
                pltpu.VMEM((columns // per_device, *block), BF16),
                pltpu.VMEM((tok_local, breadth * breadth, width), BF16),
            ],
        ),
        out_shape=jax.ShapeDtypeStruct(base.shape, BF16),
        compiler_params=pltpu.CompilerParams(
            vmem_limit_bytes=16 * 2**20 + 5 * columns * breadth * seqs * 2
        ),
        cost_estimate=pl.CostEstimate(
            flops=2 * tok_local * columns * breadth * breadth * (seqs + pair_width),
            bytes_accessed=8 * tok_local * columns * pair_width,
            transcendentals=0,
        ),
        name="pair_update",
    )(me, left, weight_t, share, base, *right_held)


def gather_stages(size):
    chips = size // 2
    high = 2 ** math.ceil(math.log2(chips) / 2)
    low = chips // high
    return [(2 * low, high), (2, low), (1, 2)]


def exchange(held, size, distance):
    return lax.ppermute(held, "wide", [(d, d ^ distance) for d in range(size)])


def gather_blocks(block, size, stages):
    (far, far_size), (near, near_size), (core, core_size) = stages
    block = block[None]
    column = jnp.concatenate(
        [block] + [exchange(block, size, f * far) for f in range(1, far_size)], axis=0
    )
    held = []
    for n in range(near_size):
        here = exchange(column, size, n * near) if n else column
        held += [here] + [exchange(here, size, c * core) for c in range(1, core_size)]
    return held


def on_device(
    size,
    homolog_stack_state,
    present_flags,
    chain_ordinal_labels,
    pairwise_repr,
    heeding_normalizer_gains,
    retrieval_weights_qkv,
    logistic_weights,
    logistic_intercept,
    emitted_weights,
    dyadic_normalizer_gains,
    former_operand_weights,
    latter_operand_weights,
    flattened_outer_projection,
    clipped_separation_embedding,
):
    me = lax.axis_index("wide")
    seq_local, columns, channels = homolog_stack_state.shape
    tok_local = pairwise_repr.shape[0]
    seqs = seq_local * size
    breadth = former_operand_weights.shape[1]
    pair_width = flattened_outer_projection.shape[1]
    stages = gather_stages(size)

    sent = homolog_stack_state.reshape(seq_local, size, tok_local, channels).transpose(1, 0, 2, 3)
    x_rows = lax.all_to_all(sent, "wide", 0, 0, tiled=True).reshape(seqs * tok_local, channels)

    flags = present_flags.astype(F32)
    mine = lax.dynamic_slice_in_dim(flags, me * tok_local, tok_local, 1)
    flag_rows = mine.T[:, None, :]
    masks = (1000000000.0 * math.sqrt(HEAD_SIZE)) * (mine - 1.0)
    bias = jnp.pad(masks, ((0, 0), (0, LANES - tok_local))).astype(BF16)
    gains = jnp.stack([heeding_normalizer_gains, dyadic_normalizer_gains])
    weights_t = retrieval_weights_qkv.T
    wqvg = jnp.concatenate(
        [weights_t[:channels], weights_t[2 * channels :], logistic_weights.T], axis=0
    )
    wk = retrieval_weights_qkv[:, channels : 2 * channels]
    wlr = jnp.concatenate([former_operand_weights.T, latter_operand_weights.T], axis=0)
    projection_t = (
        flattened_outer_projection.reshape(breadth, breadth, pair_width)
        .transpose(2, 1, 0)
        .reshape(pair_width, breadth * breadth)
    )
    counts = jnp.dot(mine.T, flags, precision=lax.Precision.HIGHEST)
    share = 1.0 / counts
    labels_mine = lax.dynamic_slice_in_dim(chain_ordinal_labels, me * tok_local, tok_local, 0)
    offsets = (
        jnp.clip(labels_mine[:, None] - chain_ordinal_labels[None, :], -RELPOS_CLIP, RELPOS_CLIP)
        + RELPOS_CLIP
    )
    span = clipped_separation_embedding.shape[0]
    one_hot = (offsets[:, :, None] == jnp.arange(span, dtype=jnp.int32)[None, None, :]).astype(BF16)
    relpos = jnp.dot(
        one_hot.reshape(tok_local * columns, span),
        clipped_separation_embedding,
        preferred_element_type=F32,
    ).reshape(tok_local, columns, pair_width)
    base = pairwise_repr.astype(F32) + relpos

    x_rows, base, share, projection_t = lax.optimization_barrier(
        (x_rows, base, share, projection_t)
    )

    changed_rows, left, right = attention(
        x_rows,
        bias,
        flag_rows,
        gains,
        wqvg,
        wk,
        logistic_intercept[:, None],
        emitted_weights,
        wlr,
        tok_local,
    )

    right_held = gather_blocks(right, size, stages)
    back = lax.all_to_all(
        changed_rows.reshape(size, seq_local, tok_local, channels), "wide", 0, 0, tiled=True
    )
    homolog_changed = back.transpose(1, 0, 2, 3).reshape(seq_local, columns, channels)
    couple_state_changed = pair_update(
        me.reshape(1), left, right_held, projection_t, share, base, stages
    )
    return (homolog_changed, couple_state_changed)


def solution(mesh):
    in_specs = (
        P(("grp", "wide"), None, None),
        P("grp", None),
        P("grp"),
        P(("grp", "wide"), None, None),
    ) + (P(),) * 10
    out_specs = (P(("grp", "wide"), None, None), P(("grp", "wide"), None, None))
    return jax.shard_map(
        functools.partial(on_device, mesh.shape["wide"]),
        mesh=mesh,
        in_specs=in_specs,
        out_specs=out_specs,
        check_vma=False,
    )
```

profile of v0, /device:TPU:0, one launch (start us, length us, event | category | flops | bytes accessed | tf_op | source)
XLA Modules:
  0.0 66.1 jit_solution(3704757331047871310)
XLA Ops:
  0.6 0.0 copy-start
  0.6 1.0 %copy-done = bf16[8,128,256]{2,1,0:T(8,128)(2,1)S(1)} copy-done((bf16[8,128,256]{2,1,0:T(8,128)(2,1)S(1)}, bf16[8,128,256]{2,1,0:T(8,128)(2,1)}, u32[]{:S(2)}) %copy-start) | copy-done | bytes 524312
  1.7 0.8 %copy_bitcast_fusion.1 = bf16[16,8,8,256]{3,2,1,0:T(8,128)(2,1)} fusion(bf16[8,128,256]{2,1,0:T(8,128)(2,1)S(1)} %copy-done), kind=kLoop, calls=%fused_computation.3 | loop fusion | bytes 1048576 | tf_op jit(solution)/shard_map/transpose | solution.py:322
  2.5 7.5 %all-to-all-start = ((bf16[16,8,8,256]{3,2,1,0:T(8,128)(2,1)}), bf16[16,8,8,256]{3,2,1,0:T(8,128)(2,1)S(1)}, u32[]{:S(2)}, u32[]{:S(2)}) async-start(bf16[16,8,8,256]{3,2,1,0:T(8,128)(2,1)} %copy_bitcast_fusion.1), calls=%async_computation | async-start | bytes 1048576 | tf_op jit(solution)/shard_map/all_to_all | solution.py:323
  10.1 0.0 copy-done.6
  10.1 0.1 copy.32
  10.2 0.2 copy.34
  10.4 0.0 copy-start.12
  10.5 0.0 copy-start.11
  10.5 0.6 copy-done.12
  11.1 0.1 copy-done.11
  11.1 0.0 copy-start.5
  11.2 0.6 copy-done.13
  11.8 0.1 dynamic_slice.6
  11.9 0.1 copy.40
  12.0 0.1 copy-done.5
  12.1 0.1 copy.35
  12.2 0.0 copy-start.10
  12.2 0.7 %copy-done.10 = f32[256]{0:T(256)S(1)} copy-done((f32[256]{0:T(256)S(1)}, f32[256]{0:T(256)}, u32[]{:S(2)}) %copy-start.10) | copy-done | bytes 1048
  12.8 0.1 copy.37.intercept_ref
  13.0 0.1 copy.33
  13.1 0.0 copy-start.8
  13.1 0.0 copy-start.9
  13.2 0.7 %copy-done.8 = bf16[256,32]{0,1:T(8,128)(2,1)S(1)} copy-done((bf16[256,32]{0,1:T(8,128)(2,1)S(1)}, bf16[256,32]{0,1:T(8,128)(2,1)}, u32[]{:S(2)}) %copy-start.8) | copy-done | bytes 16408
  13.8 0.0 copy-done.9
  13.9 0.1 clamp_add_fusion
  14.0 0.2 convolution_divide_fusion.share_ref
  14.1 0.7 %copy-done.3 = bf16[8,128,128]{2,1,0:T(8,128)(2,1)S(1)} copy-done((bf16[8,128,128]{2,1,0:T(8,128)(2,1)S(1)}, bf16[8,128,128]{2,1,0:T(8,128)(2,1)}, u32[]{:S(2)}) %copy-start.3) | copy-done | bytes 262168
  14.8 0.3 convolution_add_fusion.base_ref
  15.1 9.2 %all-to-all-done = bf16[16,8,8,256]{3,2,1,0:T(8,128)(2,1)S(1)} async-done(((bf16[16,8,8,256]{3,2,1,0:T(8,128)(2,1)}), bf16[16,8,8,256]{3,2,1,0:T(8,128)(2,1)S(1)}, u32[]{:S(2)}, u32[]{:S(2)}) %all-to-all-start) | async-done | bytes 524320 | tf_op jit(solution)/shard_map/all_to_all | solution.py:323
  24.4 4.3 %attention.1 = (bf16[1024,256]{1,0:T(8,128)(2,1)}, bf16[8,32,128]{2,1,0:T(8,128)(2,1)S(1)}, bf16[256,128]{1,0:T(8,128)(2,1)S(1)}) custom-call(bf16[1024,256]{1,0:T(8,128)(2,1)S(1)} %bitcast.32, bf16[128,128]{1,0:T(8,128)(2,1)S(1)} %pad.5.clone.bias_ref, f32[8,1,128]{2,1,0:T(1,128)S(1)} %bitcast.37, f32[2,256]{1,0:T(2,128)S(1)} %pad_maximum_fusion.3.gains_ref, ...), custom_call_target="tpu_custom_call" | custom-call | flops 805306368 | bytes 1048576 | tf_op jit(solution)/shard_map/attention/pallas_call | solution.py:164
  28.7 4.2 %all-to-all-start.1 = ((bf16[16,8,8,256]{3,2,1,0:T(8,128)(2,1)}), bf16[16,8,8,256]{3,2,1,0:T(8,128)(2,1)S(1)}, u32[]{:S(2)}, u32[]{:S(2)}) async-start(bf16[16,8,8,256]{3,2,1,0:T(8,128)(2,1)} %bitcast.16), calls=%async_computation.1 | async-start | bytes 1048576 | tf_op jit(solution)/shard_map/all_to_all | solution.py:376
  32.8 3.7 %collective-permute-start.2 = (bf16[1,256,128]{2,1,0:T(8,128)(2,1)S(1)}, bf16[1,256,128]{2,1,0:T(8,128)(2,1)S(1)}, u32[]{:S(2)}, u32[]{:S(2)}) collective-permute-start(bf16[1,256,128]{2,1,0:T(8,128)(2,1)S(1)} %bitcast.33), channel_id=1, source_target_pairs={{0,12},{1,13},{2,14},{3,15},{4,8},{5,9},{6,10},{7,11},{8,4},{9,5},... | collective-permute-start | bytes 196616 | tf_op jit(solution)/shard_map/ppermute | solution.py:281
  36.6 0.0 collective-permute-start.1
  36.6 0.7 %collective-permute-start = (bf16[1,256,128]{2,1,0:T(8,128)(2,1)S(1)}, bf16[1,256,128]{2,1,0:T(8,128)(2,1)S(1)}, u32[]{:S(2)}, u32[]{:S(2)}) collective-permute-start(bf16[1,256,128]{2,1,0:T(8,128)(2,1)S(1)} %bitcast.35), channel_id=1, source_target_pairs={{0,4},{1,5},{2,6},{3,7},{4,0},{5,1},{6,2},{7,3},{8,12},{9,13},{10,... | collective-permute-start | bytes 196616 | tf_op jit(solution)/shard_map/ppermute | solution.py:281
  37.3 10.9 %collective-permute-done.2 = bf16[1,256,128]{2,1,0:T(8,128)(2,1)S(1)} collective-permute-done((bf16[1,256,128]{2,1,0:T(8,128)(2,1)S(1)}, bf16[1,256,128]{2,1,0:T(8,128)(2,1)S(1)}, u32[]{:S(2)}, u32[]{:S(2)}) %collective-permute-start.2) | collective-permute-done | bytes 65568 | tf_op jit(solution)/shard_map/ppermute | solution.py:281
  48.2 5.5 %collective-permute-done.1 = bf16[1,256,128]{2,1,0:T(8,128)(2,1)S(1)} collective-permute-done((bf16[1,256,128]{2,1,0:T(8,128)(2,1)S(1)}, bf16[1,256,128]{2,1,0:T(8,128)(2,1)S(1)}, u32[]{:S(2)}, u32[]{:S(2)}) %collective-permute-start.1) | collective-permute-done | bytes 65568 | tf_op jit(solution)/shard_map/ppermute | solution.py:281
  53.7 0.0 collective-permute-done
  53.7 1.5 %collective-permute-start.4 = (bf16[4,256,128]{2,1,0:T(8,128)(2,1)S(1)}, bf16[4,256,128]{2,1,0:T(8,128)(2,1)S(1)}, u32[]{:S(2)}, u32[]{:S(2)}) collective-permute-start(bf16[4,256,128]{2,1,0:T(8,128)(2,1)S(1)} %pad_maximum_fusion.1.refs_0_), channel_id=1, source_target_pairs={{0,2},{1,3},{2,0},{3,1},{4,6},{5,7},{6,4},{7,5},{8,10},{9,11},{10,... | collective-permute-start | bytes 786440 | tf_op jit(solution)/shard_map/ppermute | solution.py:281
  55.3 0.0 collective-permute-start.3
  55.3 6.3 %collective-permute-done.4.refs_2_ = bf16[4,256,128]{2,1,0:T(8,128)(2,1)S(1)} collective-permute-done((bf16[4,256,128]{2,1,0:T(8,128)(2,1)S(1)}, bf16[4,256,128]{2,1,0:T(8,128)(2,1)S(1)}, u32[]{:S(2)}, u32[]{:S(2)}) %collective-permute-start.4) | collective-permute-done | bytes 262176 | tf_op jit(solution)/shard_map/ppermute | solution.py:281
  61.6 0.0 collective-permute-start.5
  61.6 0.1 copy.39.weight_ref
  61.7 0.0 collective-permute-done.3.refs_1_
  61.7 1.4 %collective-permute-done.5.refs_3_ = bf16[4,256,128]{2,1,0:T(8,128)(2,1)S(1)} collective-permute-done((bf16[4,256,128]{2,1,0:T(8,128)(2,1)S(1)}, bf16[4,256,128]{2,1,0:T(8,128)(2,1)S(1)}, u32[]{:S(2)}, u32[]{:S(2)}) %collective-permute-start.5) | collective-permute-done | bytes 262176 | tf_op jit(solution)/shard_map/ppermute | solution.py:281
  63.1 2.2 %pair_update.1 = bf16[8,128,128]{2,1,0:T(8,128)(2,1)} custom-call(s32[1]{0:T(128)} %bitcast.19.me_ref, bf16[8,32,128]{2,1,0:T(8,128)(2,1)S(1)} %get-tuple-element.11.left_ref, bf16[128,1024]{1,0:T(8,128)(2,1)S(1)} %copy.39.weight_ref, f32[8,128]{1,0:T(8,128)S(1)} %convolution_divide_fusion.share_ref, f32[8,128,128]{2,1,0:T(8,128)S(1)} %convolution_add_fusion.base_ref, ...), custom_call_target="tpu_custom_call" | custom-call | flops 536870912 | bytes 1048576 | tf_op jit(solution)/shard_map/pair_update/pallas_call | solution.py:242
  65.3 0.0 all-to-all-done.1
  65.3 0.8 %copy_bitcast_fusion = bf16[8,128,256]{2,1,0:T(8,128)(2,1)} fusion(bf16[16,8,8,256]{3,2,1,0:T(8,128)(2,1)S(1)} %all-to-all-done.1), kind=kLoop, calls=%fused_computation.2 | loop fusion | bytes 1048576 | tf_op jit(solution)/shard_map/reshape | solution.py:379
  (20 shorter events, 0.2 us)
Async XLA Ops:
  0.6 1.0 %copy-start = (bf16[8,128,256]{2,1,0:T(8,128)(2,1)S(1)}, bf16[8,128,256]{2,1,0:T(8,128)(2,1)}, u32[]{:S(2)}) copy-start(bf16[8,128,256]{2,1,0:T(8,128)(2,1)} %param.14) | copy-start | bytes 1572868
  2.5 7.6 %copy-start.6 = (s32[128,128]{1,0:T(8,128)S(1)}, s32[128,128]{1,0:T(8,128)}, u32[]{:S(2)}) copy-start(s32[128,128]{1,0:T(8,128)} %param.15) | copy-start | bytes 196612
  2.5 7.7 %copy-start.2 = (bf16[256,768]{1,0:T(8,128)(2,1)S(1)}, bf16[256,768]{1,0:T(8,128)(2,1)}, u32[]{:S(2)}) copy-start(bf16[256,768]{1,0:T(8,128)(2,1)} %param.19) | copy-start | bytes 1179652
  2.5 21.8 %all-to-all-start = ((bf16[16,8,8,256]{3,2,1,0:T(8,128)(2,1)}), bf16[16,8,8,256]{3,2,1,0:T(8,128)(2,1)S(1)}, u32[]{:S(2)}, u32[]{:S(2)}) async-start(bf16[16,8,8,256]{3,2,1,0:T(8,128)(2,1)} %copy_bitcast_fusion.1), calls=%async_computation | async-start | bytes 1048576 | tf_op jit(solution)/shard_map/all_to_all | solution.py:323
  10.4 0.7 %copy-start.12 = (f32[256]{0:T(256)S(1)}, f32[256]{0:T(256)}, u32[]{:S(2)}) copy-start(f32[256]{0:T(256)} %param.18) | copy-start | bytes 3076
  10.5 0.7 %copy-start.11 = (f32[256]{0:T(256)S(1)}, f32[256]{0:T(256)}, u32[]{:S(2)}) copy-start(f32[256]{0:T(256)} %param.23) | copy-start | bytes 3076
  11.1 0.7 copy-start.13
  11.1 0.9 %copy-start.5 = (bf16[256,256]{1,0:T(8,128)(2,1)S(1)}, bf16[256,256]{1,0:T(8,128)(2,1)}, u32[]{:S(2)}) copy-start(bf16[256,256]{1,0:T(8,128)(2,1)} %param.20) | copy-start | bytes 393220
  11.8 1.2 %copy-start.4 = (bf16[1024,128]{1,0:T(8,128)(2,1)S(1)}, bf16[1024,128]{1,0:T(8,128)(2,1)}, u32[]{:S(2)}) copy-start(bf16[1024,128]{1,0:T(8,128)(2,1)} %param.26) | copy-start | bytes 786436
  12.2 0.7 %copy-start.10 = (f32[256]{0:T(256)S(1)}, f32[256]{0:T(256)}, u32[]{:S(2)}) copy-start(f32[256]{0:T(256)} %param.21) | copy-start | bytes 3076
  13.1 0.7 %copy-start.8 = (bf16[256,32]{0,1:T(8,128)(2,1)S(1)}, bf16[256,32]{0,1:T(8,128)(2,1)}, u32[]{:S(2)}) copy-start(bf16[256,32]{0,1:T(8,128)(2,1)} %param.25) | copy-start | bytes 49156
  13.1 0.7 %copy-start.9 = (bf16[256,32]{0,1:T(8,128)(2,1)S(1)}, bf16[256,32]{0,1:T(8,128)(2,1)}, u32[]{:S(2)}) copy-start(bf16[256,32]{0,1:T(8,128)(2,1)} %param.24) | copy-start | bytes 49156
  13.9 0.9 %copy-start.3 = (bf16[8,128,128]{2,1,0:T(8,128)(2,1)S(1)}, bf16[8,128,128]{2,1,0:T(8,128)(2,1)}, u32[]{:S(2)}) copy-start(bf16[8,128,128]{2,1,0:T(8,128)(2,1)} %param.17) | copy-start | bytes 786436
  14.0 0.8 %copy-start.7 = (bf16[65,128]{1,0:T(8,128)(2,1)S(1)}, bf16[65,128]{1,0:T(8,128)(2,1)}, u32[]{:S(2)}) copy-start(bf16[65,128]{1,0:T(8,128)(2,1)} %param.27) | copy-start | bytes 49924
  14.8 9.5 %copy-start.1 = (bf16[256,256]{1,0:T(8,128)(2,1)S(1)}, bf16[256,256]{1,0:T(8,128)(2,1)}, u32[]{:S(2)}) copy-start(bf16[256,256]{1,0:T(8,128)(2,1)} %wo_ref.1) | copy-start | bytes 393220
  28.7 36.6 %all-to-all-start.1 = ((bf16[16,8,8,256]{3,2,1,0:T(8,128)(2,1)}), bf16[16,8,8,256]{3,2,1,0:T(8,128)(2,1)S(1)}, u32[]{:S(2)}, u32[]{:S(2)}) async-start(bf16[16,8,8,256]{3,2,1,0:T(8,128)(2,1)} %bitcast.16), calls=%async_computation.1 | async-start | bytes 1048576 | tf_op jit(solution)/shard_map/all_to_all | solution.py:376
  32.8 15.3 %collective-permute-start.2 = (bf16[1,256,128]{2,1,0:T(8,128)(2,1)S(1)}, bf16[1,256,128]{2,1,0:T(8,128)(2,1)S(1)}, u32[]{:S(2)}, u32[]{:S(2)}) collective-permute-start(bf16[1,256,128]{2,1,0:T(8,128)(2,1)S(1)} %bitcast.33), channel_id=1, source_target_pairs={{0,12},{1,13},{2,14},{3,15},{4,8},{5,9},{6,10},{7,11},{8,4},{9,5},... | collective-permute-start | bytes 196616 | tf_op jit(solution)/shard_map/ppermute | solution.py:281
  36.6 17.1 %collective-permute-start.1 = (bf16[1,256,128]{2,1,0:T(8,128)(2,1)S(1)}, bf16[1,256,128]{2,1,0:T(8,128)(2,1)S(1)}, u32[]{:S(2)}, u32[]{:S(2)}) collective-permute-start(bf16[1,256,128]{2,1,0:T(8,128)(2,1)S(1)} %bitcast.34), channel_id=1, source_target_pairs={{0,8},{1,9},{2,10},{3,11},{4,12},{5,13},{6,14},{7,15},{8,0},{9,1},... | collective-permute-start | bytes 196616 | tf_op jit(solution)/shard_map/ppermute | solution.py:281
  36.6 17.1 %collective-permute-start = (bf16[1,256,128]{2,1,0:T(8,128)(2,1)S(1)}, bf16[1,256,128]{2,1,0:T(8,128)(2,1)S(1)}, u32[]{:S(2)}, u32[]{:S(2)}) collective-permute-start(bf16[1,256,128]{2,1,0:T(8,128)(2,1)S(1)} %bitcast.35), channel_id=1, source_target_pairs={{0,4},{1,5},{2,6},{3,7},{4,0},{5,1},{6,2},{7,3},{8,12},{9,13},{10,... | collective-permute-start | bytes 196616 | tf_op jit(solution)/shard_map/ppermute | solution.py:281
  53.7 7.8 %collective-permute-start.4 = (bf16[4,256,128]{2,1,0:T(8,128)(2,1)S(1)}, bf16[4,256,128]{2,1,0:T(8,128)(2,1)S(1)}, u32[]{:S(2)}, u32[]{:S(2)}) collective-permute-start(bf16[4,256,128]{2,1,0:T(8,128)(2,1)S(1)} %pad_maximum_fusion.1.refs_0_), channel_id=1, source_target_pairs={{0,2},{1,3},{2,0},{3,1},{4,6},{5,7},{6,4},{7,5},{8,10},{9,11},{10,... | collective-permute-start | bytes 786440 | tf_op jit(solution)/shard_map/ppermute | solution.py:281
  55.3 6.4 %collective-permute-start.3 = (bf16[4,256,128]{2,1,0:T(8,128)(2,1)S(1)}, bf16[4,256,128]{2,1,0:T(8,128)(2,1)S(1)}, u32[]{:S(2)}, u32[]{:S(2)}) collective-permute-start(bf16[4,256,128]{2,1,0:T(8,128)(2,1)S(1)} %pad_maximum_fusion.1.refs_0_), channel_id=1, source_target_pairs={{0,1},{1,0},{2,3},{3,2},{4,5},{5,4},{6,7},{7,6},{8,9},{9,8},{10,11... | collective-permute-start | bytes 786440 | tf_op jit(solution)/shard_map/ppermute | solution.py:281
  61.6 1.5 %collective-permute-start.5 = (bf16[4,256,128]{2,1,0:T(8,128)(2,1)S(1)}, bf16[4,256,128]{2,1,0:T(8,128)(2,1)S(1)}, u32[]{:S(2)}, u32[]{:S(2)}) collective-permute-start(bf16[4,256,128]{2,1,0:T(8,128)(2,1)S(1)} %collective-permute-done.4.refs_2_), channel_id=1, source_target_pairs={{0,1},{1,0},{2,3},{3,2},{4,5},{5,4},{6,7},{7,6},{8,9},{9,8},{10,11... | collective-permute-start | bytes 786440 | tf_op jit(solution)/shard_map/ppermute | solution.py:281
where the time goes:
time: 66.6 us; the launch traced here: 66.1 us
  waiting for transfers between devices  33.3 us (50%)
  starting transfers between devices  17.7 us (27%)
  local copies, waits for them, and re-layouts  7.12 us (11%)
  Pallas kernels  6.49 us (10%)
  between operations  0.85 us (1%)
    ppermute x6, waiting for transfers between devices, exchange(): return lax.ppermute(held, 'wide', [(d, d ^ distance) for d in range(size)])  24.1 us
    all_to_all x1, waiting for transfers between devices, on_device(): lax.all_to_all(sent, 'wide', 0, 0, tiled=True)  9.21 us
    all_to_all x1, starting transfers between devices, on_device(): lax.all_to_all(sent, 'wide', 0, 0, tiled=True)  7.55 us
    ppermute x6, starting transfers between devices, exchange(): return lax.ppermute(held, 'wide', [(d, d ^ distance) for d in range(size)])  5.99 us
    unnamed x32, local copies, waits for them, and re-layouts  4.95 us
    pallas_call x1, Pallas kernels, attention(): pl.pallas_call(functools.partial(attention_kernel, tokens), out_shape=(ja...  4.32 us
    all_to_all x1, starting transfers between devices, on_device(): lax.all_to_all(changed_rows.reshape(size, seq_local, tok_local, channels)...  4.16 us
    pallas_call x1, Pallas kernels, pair_update(): pl.pallas_call(functools.partial(pair_kernel, stages, per_device), grid_s...  2.17 us
  transfers between devices with their start and end apart: 8, of which 5 were waited for; matrix products, arithmetic and copies ran while one was open for 2% of the time, Pallas kernels for 3%

commit v1 on v0

--- a/solution.py
+++ b/solution.py
@@ -197,77 +197,140 @@
 
 
 def pair_kernel(
-    stages, per_device, me_ref, left_ref, weight_ref, share_ref, base_ref, *refs
+    stages, distance, me_ref, left_ref, weight_ref, share_ref, base_ref, *refs
 ):
-    held_refs, (out_ref, right_ref, outer_ref) = refs[:-3], refs[-3:]
+    (far, far_size), (near, near_size), (core, core_size) = stages
+    held_refs, refs = refs[:core_size], refs[core_size:]
+    last = distance == near_size - 1
+    if last:
+        done_refs, refs = refs[:-8], refs[-8:]
+        back_ref, out_ref, changed_ref, right_ref, outer_ref, whole_ref, pair_ref, sems = refs
+        devices, sequences = back_ref.shape[:2]
+        for d in range(devices):
+            for n in range(sequences):
+                whole_ref[n, d] = back_ref[d, n]
+        copies = [pltpu.make_async_copy(whole_ref, changed_ref, sems.at[left_ref.shape[0]])]
+        copies[0].start()
+    else:
+        done_refs, (out_ref, right_ref, outer_ref) = (), refs
     tok_local, breadth, seqs = left_ref.shape
-    width = out_ref.shape[1]
-    first = pl.program_id(0) * (width // per_device)
+    per_device = held_refs[0].shape[1] // breadth
+    chunk = core_size * per_device
+    width = far_size * chunk
+    pack = max(1, LANES // width)
     me = me_ref[0]
-    (far, far_size), (near, near_size), (core, core_size) = stages
-
-    @pl.when(pl.program_id(0) == 0)
-    def _():
-        for n in range(near_size):
-            for c in range(core_size):
+    my_far = jnp.bitwise_and(me // far, far_size - 1)
+    my_near = jnp.bitwise_and(me // near, near_size - 1)
+    my_core = jnp.bitwise_and(me // core, core_size - 1)
+
+    def rows_at(f, n):
+        chip = f * near_size + jnp.bitwise_xor(my_near, n)
+        return pl.ds(pl.multiple_of(chip * chunk, chunk), chunk)
+
+    for c in range(core_size):
+        for f in range(far_size):
+            device = jnp.bitwise_xor(my_far, f) * core_size + jnp.bitwise_xor(my_core, c)
+            right_ref[device] = held_refs[c][f]
+
+    left = left_ref[...].reshape(tok_local // pack, pack, breadth, seqs)
+    left = jnp.concatenate(
+        [left[:, k].reshape(tok_local // pack * breadth, seqs) for k in range(pack)], axis=1
+    )
+    nothing = jnp.zeros((width, seqs), BF16)
+    step = 2 if breadth % 2 == 0 else 1
+    for e in range(0, breadth, step):
+        rows = []
+        for k in range(e, e + step):
+            right = jnp.concatenate(
+                [
+                    right_ref[d, k * per_device : (k + 1) * per_device, :]
+                    for d in range(far_size * core_size)
+                ],
+                axis=0,
+            )
+            rows += [
+                jnp.concatenate([right if j == k2 else nothing for j in range(pack)], axis=1)
+                for k2 in range(pack)
+            ]
+        outer = lax.dot_general(
+            left, jnp.concatenate(rows, axis=0), NT, preferred_element_type=F32
+        ).astype(BF16)
+        lanes = pack * width
+        for k in range(step):
+            outer_ref[:, (e + k) * breadth : (e + k + 1) * breadth, :] = outer[
+                :, k * lanes : (k + 1) * lanes
+            ].reshape(tok_local // pack, breadth, lanes)
+
+    share = share_ref[jnp.bitwise_xor(my_near, distance)]
+    for q in range(tok_local // pack):
+        projected = jnp.dot(weight_ref[...], outer_ref[q], preferred_element_type=F32)
+        projected = (projected * share[q : q + 1]).T
+        for k in range(pack):
+            i = q * pack + k
+            for f in range(far_size):
+                here = rows_at(f, distance)
+                mine = projected[k * width + f * chunk : k * width + (f + 1) * chunk]
+                value = (base_ref[i, here, :] + mine).astype(BF16)
+                if last:
+                    pair_ref[i, here, :] = value
+                else:
+                    out_ref[i, f * chunk : (f + 1) * chunk, :] = value
+            for n, done_ref in enumerate(done_refs):
                 for f in range(far_size):
-                    device = jnp.bitwise_xor(me, f * far + n * near + c * core)
-                    right_ref[device] = held_refs[n * core_size + c][f]
-
-    left = left_ref[...].reshape(tok_local * breadth, seqs)
-    for e in range(breadth):
-        right = jnp.concatenate(
-            [
-                right_ref[first + d, e * per_device : (e + 1) * per_device, :]
-                for d in range(width // per_device)
-            ],
-            axis=0,
-        )
-        outer = lax.dot_general(left, right, NT, preferred_element_type=F32).astype(BF16)
-        outer_ref[:, e * breadth : (e + 1) * breadth, :] = outer.reshape(tok_local, breadth, width)
-
-    for i in range(tok_local):
-        projected = jnp.dot(weight_ref[...], outer_ref[i], preferred_element_type=F32)
-        projected = projected * share_ref[i : i + 1, :]
-        out_ref[i] = (base_ref[i] + projected.T).astype(BF16)
-
-
-def pair_update(me, left, right_held, weight_t, share, base, stages):
+                    pair_ref[i, rows_at(f, n), :] = done_ref[i, f * chunk : (f + 1) * chunk, :]
+            if last:
+                copies.append(pltpu.make_async_copy(pair_ref.at[i], out_ref.at[i], sems.at[i]))
+                copies[-1].start()
+    if last:
+        for copy in copies:
+            copy.wait()
+
+
+def pair_part(distance, me, left, weight_t, share, base, held, done, back, stages):
     tok_local, breadth, seqs = left.shape
     pair_width = weight_t.shape[0]
-    block = right_held[0].shape[1:]
-    per_device = block[0] // breadth
+    far_size, block = held[0].shape[0], held[0].shape[1:]
     columns = base.shape[1]
-    width = min(columns, LANES)
+    width = columns // stages[1][1]
+    pack = max(1, LANES // width)
+    size, seq_local, _, channels = back.shape
+    last = distance == stages[1][1] - 1
+    vmem = pl.BlockSpec(memory_space=pltpu.VMEM)
+    scratch = [
+        pltpu.VMEM((far_size * len(held), *block), BF16),
+        pltpu.VMEM((tok_local // pack, breadth * breadth, pack * width), BF16),
+    ]
+    out_shape = jax.ShapeDtypeStruct((tok_local, width, pair_width), BF16)
+    out_specs = vmem
+    operands = [left, weight_t, share, base, *held]
+    if last:
+        operands += [*done, back]
+        out_shape = (
+            jax.ShapeDtypeStruct(base.shape, BF16),
+            jax.ShapeDtypeStruct((seq_local, size, tok_local, channels), BF16),
+        )
+        out_specs = (pl.BlockSpec(memory_space=pl.ANY), pl.BlockSpec(memory_space=pl.ANY))
+        scratch += [
+            pltpu.VMEM((seq_local, size, tok_local, channels), BF16),
+            pltpu.VMEM(base.shape, BF16),
+            pltpu.SemaphoreType.DMA((tok_local + 1,)),
+        ]
     return pl.pallas_call(
-        functools.partial(pair_kernel, stages, per_device),
-        grid_spec=pltpu.PrefetchScalarGridSpec(
-            num_scalar_prefetch=1,
-            grid=(columns // width,),
-            in_specs=[
-                pl.BlockSpec(left.shape, lambda j, me: (0, 0, 0)),
-                pl.BlockSpec(weight_t.shape, lambda j, me: (0, 0)),
-                pl.BlockSpec((tok_local, width), lambda j, me: (0, j)),
-                pl.BlockSpec((tok_local, width, pair_width), lambda j, me: (0, j, 0)),
-            ]
-            + [pl.BlockSpec(held.shape, lambda j, me: (0, 0, 0)) for held in right_held],
-            out_specs=pl.BlockSpec((tok_local, width, pair_width), lambda j, me: (0, j, 0)),
-            scratch_shapes=[
-                pltpu.VMEM((columns // per_device, *block), BF16),
-                pltpu.VMEM((tok_local, breadth * breadth, width), BF16),
-            ],
-        ),
-        out_shape=jax.ShapeDtypeStruct(base.shape, BF16),
+        functools.partial(pair_kernel, stages, distance),
+        in_specs=[pl.BlockSpec(memory_space=pltpu.SMEM)] + [vmem] * len(operands),
+        out_specs=out_specs,
+        scratch_shapes=scratch,
+        out_shape=out_shape,
         compiler_params=pltpu.CompilerParams(
-            vmem_limit_bytes=16 * 2**20 + 5 * columns * breadth * seqs * 2
+            vmem_limit_bytes=16 * 2**20 + 12 * tok_local * columns * pair_width
         ),
         cost_estimate=pl.CostEstimate(
-            flops=2 * tok_local * columns * breadth * breadth * (seqs + pair_width),
-            bytes_accessed=8 * tok_local * columns * pair_width,
+            flops=2 * tok_local * width * breadth * breadth * (seqs + pair_width),
+            bytes_accessed=8 * tok_local * width * pair_width,
             transcendentals=0,
         ),
-        name="pair_update",
-    )(me, left, weight_t, share, base, *right_held)
+        name="pair_part",
+    )(me, *operands)
 
 
 def gather_stages(size):
@@ -290,7 +353,7 @@
     held = []
     for n in range(near_size):
         here = exchange(column, size, n * near) if n else column
-        held += [here] + [exchange(here, size, c * core) for c in range(1, core_size)]
+        held.append([here] + [exchange(here, size, c * core) for c in range(1, core_size)])
     return held
 
 
@@ -340,7 +403,10 @@
         .reshape(pair_width, breadth * breadth)
     )
     counts = jnp.dot(mine.T, flags, precision=lax.Precision.HIGHEST)
-    share = 1.0 / counts
+    far_size, near_size = stages[0][1], stages[1][1]
+    pack = max(1, LANES * near_size // columns)
+    share = (1.0 / counts).reshape(tok_local, far_size, near_size, -1).transpose(2, 0, 1, 3)
+    share = share.reshape(near_size, tok_local // pack, pack * columns // near_size)
     labels_mine = lax.dynamic_slice_in_dim(chain_ordinal_labels, me * tok_local, tok_local, 0)
     offsets = (
         jnp.clip(labels_mine[:, None] - chain_ordinal_labels[None, :], -RELPOS_CLIP, RELPOS_CLIP)
@@ -376,11 +442,23 @@
     back = lax.all_to_all(
         changed_rows.reshape(size, seq_local, tok_local, channels), "wide", 0, 0, tiled=True
     )
-    homolog_changed = back.transpose(1, 0, 2, 3).reshape(seq_local, columns, channels)
-    couple_state_changed = pair_update(
-        me.reshape(1), left, right_held, projection_t, share, base, stages
-    )
-    return (homolog_changed, couple_state_changed)
+    done = []
+    for distance, held in enumerate(right_held):
+        part = pair_part(
+            distance,
+            me.reshape(1),
+            left,
+            projection_t,
+            share,
+            base,
+            held,
+            done[:],
+            back,
+            stages,
+        )
+        done.append(part)
+    couple_state_changed, homolog_changed = done[-1]
+    return (homolog_changed.reshape(seq_local, columns, channels), couple_state_changed)
 
 
 def solution(mesh):

time: 66.6 us -> 65.7 us (0.986)
  waiting for transfers between devices: 33.3 us -> 31.3 us
  Pallas kernels: 6.49 us -> 7.7 us
    ppermute x6, waiting for transfers between devices: 24.1 us -> 22.8 us  [exchange(): return lax.ppermute(held, 'wide', [(d, d ^ distance) for d in range(size)])]
    pallas_call x1 -> x2, Pallas kernels: 2.17 us -> 3.39 us  [pair_part(): pl.pallas_call(functools.partial(pair_kernel, stages, distance), in_specs...]
    all_to_all x1, waiting for transfers between devices: 9.21 us -> 8.51 us  [on_device(): lax.all_to_all(sent, 'wide', 0, 0, tiled=True)]
  transfers between devices with their start and end apart: 8 -> 8, of which waited for: 5 -> 5; matrix products, arithmetic and copies ran while one was open for 2% -> 3% of each run, Pallas kernels for 3% -> 2%
where the time goes in v1:
time: 65.7 us; the launch traced here: 65.2 us
  waiting for transfers between devices  31.3 us (48%)
  starting transfers between devices  17.7 us (27%)
  Pallas kernels  7.7 us (12%)
  local copies, waits for them, and re-layouts  6.98 us (11%)
  between operations  0.87 us (1%)
    ppermute x6, waiting for transfers between devices, exchange(): return lax.ppermute(held, 'wide', [(d, d ^ distance) for d in range(size)])  22.8 us
    all_to_all x1, waiting for transfers between devices, on_device(): lax.all_to_all(sent, 'wide', 0, 0, tiled=True)  8.51 us
    all_to_all x1, starting transfers between devices, on_device(): lax.all_to_all(sent, 'wide', 0, 0, tiled=True)  7.55 us
    ppermute x6, starting transfers between devices, exchange(): return lax.ppermute(held, 'wide', [(d, d ^ distance) for d in range(size)])  5.99 us
    unnamed x32, local copies, waits for them, and re-layouts  5.44 us
    pallas_call x1, Pallas kernels, attention(): pl.pallas_call(functools.partial(attention_kernel, tokens), out_shape=(ja...  4.32 us
    all_to_all x1, starting transfers between devices, on_device(): lax.all_to_all(changed_rows.reshape(size, seq_local, tok_local, channels)...  4.17 us
    pallas_call x2, Pallas kernels, pair_part(): pl.pallas_call(functools.partial(pair_kernel, stages, distance), in_specs...  3.39 us
  transfers between devices with their start and end apart: 8, of which 5 were waited for; matrix products, arithmetic and copies ran while one was open for 3% of the time, Pallas kernels for 2%

profile of v1, /device:TPU:0, one launch (start us, length us, event | category | flops | bytes accessed | tf_op | source)
XLA Modules:
  0.0 65.2 jit_solution(3270838584059293853)
XLA Ops:
  0.6 0.0 copy-start
  0.6 1.0 %copy-done = bf16[8,128,256]{2,1,0:T(8,128)(2,1)S(1)} copy-done((bf16[8,128,256]{2,1,0:T(8,128)(2,1)S(1)}, bf16[8,128,256]{2,1,0:T(8,128)(2,1)}, u32[]{:S(2)}) %copy-start) | copy-done | bytes 524312
  1.7 0.8 %copy_bitcast_fusion = bf16[16,8,8,256]{3,2,1,0:T(8,128)(2,1)} fusion(bf16[8,128,256]{2,1,0:T(8,128)(2,1)S(1)} %copy-done), kind=kLoop, calls=%fused_computation.2 | loop fusion | bytes 1048576 | tf_op jit(solution)/shard_map/transpose | solution.py:385
  2.5 7.5 %all-to-all-start = ((bf16[16,8,8,256]{3,2,1,0:T(8,128)(2,1)}), bf16[16,8,8,256]{3,2,1,0:T(8,128)(2,1)S(1)}, u32[]{:S(2)}, u32[]{:S(2)}) async-start(bf16[16,8,8,256]{3,2,1,0:T(8,128)(2,1)} %copy_bitcast_fusion), calls=%async_computation | async-start | bytes 1048576 | tf_op jit(solution)/shard_map/all_to_all | solution.py:386
  10.1 0.1 copy.33
  10.2 0.0 copy-start.12
  10.2 0.2 convolution_divide_fusion
  10.4 0.5 copy-done.12
  10.9 0.2 copy-done.11
  11.2 0.0 copy-start.13
  11.2 0.2 copy.36
  11.4 0.5 copy-done.13
  11.8 0.1 dynamic_slice.6
  11.9 0.1 reshape.77
  12.0 0.0 copy-start.4
  12.0 0.1 reshape.78.share_ref
  12.1 0.1 copy.42
  12.3 0.5 copy-done.5
  12.7 0.1 copy.37
  12.8 0.0 copy-start.10
  12.9 0.7 %copy-done.10 = f32[256]{0:T(256)S(1)} copy-done((f32[256]{0:T(256)S(1)}, f32[256]{0:T(256)}, u32[]{:S(2)}) %copy-start.10) | copy-done | bytes 1048
  13.5 0.1 copy.39.intercept_ref
  13.7 0.1 copy.35
  13.8 0.0 copy-start.8
  13.8 0.0 copy-start.9
  13.8 0.7 %copy-done.8 = bf16[256,32]{0,1:T(8,128)(2,1)S(1)} copy-done((bf16[256,32]{0,1:T(8,128)(2,1)S(1)}, bf16[256,32]{0,1:T(8,128)(2,1)}, u32[]{:S(2)}) %copy-start.8) | copy-done | bytes 16408
  14.5 0.0 copy-done.9
  14.6 0.0 copy-start.3
  14.6 0.0 copy-start.7
  14.6 0.1 clamp_add_fusion
  14.7 0.8 %copy-done.3 = bf16[8,128,128]{2,1,0:T(8,128)(2,1)S(1)} copy-done((bf16[8,128,128]{2,1,0:T(8,128)(2,1)S(1)}, bf16[8,128,128]{2,1,0:T(8,128)(2,1)}, u32[]{:S(2)}) %copy-start.3) | copy-done | bytes 262168
  15.5 0.3 convolution_add_fusion.base_ref
  15.8 8.5 %all-to-all-done = bf16[16,8,8,256]{3,2,1,0:T(8,128)(2,1)S(1)} async-done(((bf16[16,8,8,256]{3,2,1,0:T(8,128)(2,1)}), bf16[16,8,8,256]{3,2,1,0:T(8,128)(2,1)S(1)}, u32[]{:S(2)}, u32[]{:S(2)}) %all-to-all-start) | async-done | bytes 524320 | tf_op jit(solution)/shard_map/all_to_all | solution.py:386
  24.4 4.3 %attention.1 = (bf16[1024,256]{1,0:T(8,128)(2,1)}, bf16[8,32,128]{2,1,0:T(8,128)(2,1)S(1)}, bf16[256,128]{1,0:T(8,128)(2,1)S(1)}) custom-call(bf16[1024,256]{1,0:T(8,128)(2,1)S(1)} %bitcast.31, bf16[128,128]{1,0:T(8,128)(2,1)S(1)} %pad.5.clone.bias_ref, f32[8,1,128]{2,1,0:T(1,128)S(1)} %bitcast.36, f32[2,256]{1,0:T(2,128)S(1)} %pad_maximum_fusion.3.gains_ref, ...), custom_call_target="tpu_custom_call" | custom-call | flops 805306368 | bytes 1048576 | tf_op jit(solution)/shard_map/attention/pallas_call | solution.py:164
  28.7 4.2 %all-to-all-start.1 = ((bf16[16,8,8,256]{3,2,1,0:T(8,128)(2,1)}), bf16[16,8,8,256]{3,2,1,0:T(8,128)(2,1)S(1)}, u32[]{:S(2)}, u32[]{:S(2)}) async-start(bf16[16,8,8,256]{3,2,1,0:T(8,128)(2,1)} %bitcast.19), calls=%async_computation.1 | async-start | bytes 1048576 | tf_op jit(solution)/shard_map/all_to_all | solution.py:442
  32.8 3.7 %collective-permute-start.2 = (bf16[1,256,128]{2,1,0:T(8,128)(2,1)S(1)}, bf16[1,256,128]{2,1,0:T(8,128)(2,1)S(1)}, u32[]{:S(2)}, u32[]{:S(2)}) collective-permute-start(bf16[1,256,128]{2,1,0:T(8,128)(2,1)S(1)} %bitcast.32), channel_id=1, source_target_pairs={{0,12},{1,13},{2,14},{3,15},{4,8},{5,9},{6,10},{7,11},{8,4},{9,5},... | collective-permute-start | bytes 196616 | tf_op jit(solution)/shard_map/ppermute | solution.py:344
  36.6 0.7 %collective-permute-start = (bf16[1,256,128]{2,1,0:T(8,128)(2,1)S(1)}, bf16[1,256,128]{2,1,0:T(8,128)(2,1)S(1)}, u32[]{:S(2)}, u32[]{:S(2)}) collective-permute-start(bf16[1,256,128]{2,1,0:T(8,128)(2,1)S(1)} %bitcast.34), channel_id=1, source_target_pairs={{0,4},{1,5},{2,6},{3,7},{4,0},{5,1},{6,2},{7,3},{8,12},{9,13},{10,... | collective-permute-start | bytes 196616 | tf_op jit(solution)/shard_map/ppermute | solution.py:344
  37.3 10.9 %collective-permute-done.2 = bf16[1,256,128]{2,1,0:T(8,128)(2,1)S(1)} collective-permute-done((bf16[1,256,128]{2,1,0:T(8,128)(2,1)S(1)}, bf16[1,256,128]{2,1,0:T(8,128)(2,1)S(1)}, u32[]{:S(2)}, u32[]{:S(2)}) %collective-permute-start.2) | collective-permute-done | bytes 65568 | tf_op jit(solution)/shard_map/ppermute | solution.py:344
  48.2 5.5 %collective-permute-done.1 = bf16[1,256,128]{2,1,0:T(8,128)(2,1)S(1)} collective-permute-done((bf16[1,256,128]{2,1,0:T(8,128)(2,1)S(1)}, bf16[1,256,128]{2,1,0:T(8,128)(2,1)S(1)}, u32[]{:S(2)}, u32[]{:S(2)}) %collective-permute-start.1) | collective-permute-done | bytes 65568 | tf_op jit(solution)/shard_map/ppermute | solution.py:344
  53.7 0.0 collective-permute-done
  53.7 1.5 %collective-permute-start.3 = (bf16[4,256,128]{2,1,0:T(8,128)(2,1)S(1)}, bf16[4,256,128]{2,1,0:T(8,128)(2,1)S(1)}, u32[]{:S(2)}, u32[]{:S(2)}) collective-permute-start(bf16[4,256,128]{2,1,0:T(8,128)(2,1)S(1)} %pad_maximum_fusion.1.refs_0_), channel_id=1, source_target_pairs={{0,2},{1,3},{2,0},{3,1},{4,6},{5,7},{6,4},{7,5},{8,10},{9,11},{10,... | collective-permute-start | bytes 786440 | tf_op jit(solution)/shard_map/ppermute | solution.py:344
  55.3 6.3 %collective-permute-done.3.refs_0_ = bf16[4,256,128]{2,1,0:T(8,128)(2,1)S(1)} collective-permute-done((bf16[4,256,128]{2,1,0:T(8,128)(2,1)S(1)}, bf16[4,256,128]{2,1,0:T(8,128)(2,1)S(1)}, u32[]{:S(2)}, u32[]{:S(2)}) %collective-permute-start.3) | collective-permute-done | bytes 262176 | tf_op jit(solution)/shard_map/ppermute | solution.py:344
  61.6 0.0 collective-permute-start.4
  61.6 0.1 copy.41.weight_ref
  61.7 0.0 collective-permute-done.5.refs_1_
  61.7 1.3 %pair_part.2.refs_2_ = bf16[8,64,128]{2,1,0:T(8,128)(2,1)S(1)} custom-call(s32[1]{0:T(128)} %bitcast.me_ref, bf16[8,32,128]{2,1,0:T(8,128)(2,1)S(1)} %get-tuple-element.12.left_ref, bf16[128,1024]{1,0:T(8,128)(2,1)S(1)} %copy.41.weight_ref, f32[2,4,128]{2,1,0:T(4,128)S(1)} %reshape.78.share_ref, f32[8,128,128]{2,1,0:T(8,128)S(1)} %convolution_add_fusion.base_ref, ...), custom_call_target="tpu_custom_call" | custom-call | flops 268435456 | bytes 524288 | tf_op jit(solution)/shard_map/pair_part/pallas_call | solution.py:318
  63.0 0.1 collective-permute-done.4.refs_1_
  63.1 2.1 %pair_part.3 = (bf16[8,128,128]{2,1,0:T(8,128)(2,1)}, bf16[8,16,8,256]{3,2,1,0:T(8,128)(2,1)}) custom-call(s32[1]{0:T(128)} %bitcast.me_ref, bf16[8,32,128]{2,1,0:T(8,128)(2,1)S(1)} %get-tuple-element.12.left_ref, bf16[128,1024]{1,0:T(8,128)(2,1)S(1)} %copy.41.weight_ref, f32[2,4,128]{2,1,0:T(4,128)S(1)} %reshape.78.share_ref, ...), custom_call_target="tpu_custom_call" | custom-call | flops 268435456 | bytes 524288 | tf_op jit(solution)/shard_map/pair_part/pallas_call | solution.py:318
  (23 shorter events, 0.2 us)
Async XLA Ops:
  0.6 1.0 %copy-start = (bf16[8,128,256]{2,1,0:T(8,128)(2,1)S(1)}, bf16[8,128,256]{2,1,0:T(8,128)(2,1)}, u32[]{:S(2)}) copy-start(bf16[8,128,256]{2,1,0:T(8,128)(2,1)} %param.14) | copy-start | bytes 1572868
  2.5 7.6 %copy-start.6 = (s32[128,128]{1,0:T(8,128)S(1)}, s32[128,128]{1,0:T(8,128)}, u32[]{:S(2)}) copy-start(s32[128,128]{1,0:T(8,128)} %param.15) | copy-start | bytes 196612
  2.5 8.6 %copy-start.2 = (bf16[256,768]{1,0:T(8,128)(2,1)S(1)}, bf16[256,768]{1,0:T(8,128)(2,1)}, u32[]{:S(2)}) copy-start(bf16[256,768]{1,0:T(8,128)(2,1)} %param.19) | copy-start | bytes 1179652
  2.5 21.8 %all-to-all-start = ((bf16[16,8,8,256]{3,2,1,0:T(8,128)(2,1)}), bf16[16,8,8,256]{3,2,1,0:T(8,128)(2,1)S(1)}, u32[]{:S(2)}, u32[]{:S(2)}) async-start(bf16[16,8,8,256]{3,2,1,0:T(8,128)(2,1)} %copy_bitcast_fusion), calls=%async_computation | async-start | bytes 1048576 | tf_op jit(solution)/shard_map/all_to_all | solution.py:386
  10.2 0.7 %copy-start.12 = (f32[256]{0:T(256)S(1)}, f32[256]{0:T(256)}, u32[]{:S(2)}) copy-start(f32[256]{0:T(256)} %param.18) | copy-start | bytes 3076
  10.4 0.7 %copy-start.11 = (f32[256]{0:T(256)S(1)}, f32[256]{0:T(256)}, u32[]{:S(2)}) copy-start(f32[256]{0:T(256)} %param.23) | copy-start | bytes 3076
  11.2 0.7 %copy-start.13 = (s32[128]{0:T(128)S(1)}, s32[128]{0:T(128)}, u32[]{:S(2)}) copy-start(s32[128]{0:T(128)} %param.16) | copy-start | bytes 1540
  11.8 0.9 %copy-start.5 = (bf16[256,256]{1,0:T(8,128)(2,1)S(1)}, bf16[256,256]{1,0:T(8,128)(2,1)}, u32[]{:S(2)}) copy-start(bf16[256,256]{1,0:T(8,128)(2,1)} %param.20) | copy-start | bytes 393220
  12.0 1.7 %copy-start.4 = (bf16[1024,128]{1,0:T(8,128)(2,1)S(1)}, bf16[1024,128]{1,0:T(8,128)(2,1)}, u32[]{:S(2)}) copy-start(bf16[1024,128]{1,0:T(8,128)(2,1)} %param.26) | copy-start | bytes 786436
  12.8 0.7 %copy-start.10 = (f32[256]{0:T(256)S(1)}, f32[256]{0:T(256)}, u32[]{:S(2)}) copy-start(f32[256]{0:T(256)} %param.21) | copy-start | bytes 3076
  13.8 0.7 %copy-start.8 = (bf16[256,32]{0,1:T(8,128)(2,1)S(1)}, bf16[256,32]{0,1:T(8,128)(2,1)}, u32[]{:S(2)}) copy-start(bf16[256,32]{0,1:T(8,128)(2,1)} %param.25) | copy-start | bytes 49156
  13.8 0.7 %copy-start.9 = (bf16[256,32]{0,1:T(8,128)(2,1)S(1)}, bf16[256,32]{0,1:T(8,128)(2,1)}, u32[]{:S(2)}) copy-start(bf16[256,32]{0,1:T(8,128)(2,1)} %param.24) | copy-start | bytes 49156
  14.6 1.0 %copy-start.3 = (bf16[8,128,128]{2,1,0:T(8,128)(2,1)S(1)}, bf16[8,128,128]{2,1,0:T(8,128)(2,1)}, u32[]{:S(2)}) copy-start(bf16[8,128,128]{2,1,0:T(8,128)(2,1)} %param.17) | copy-start | bytes 786436
  14.6 0.9 %copy-start.7 = (bf16[65,128]{1,0:T(8,128)(2,1)S(1)}, bf16[65,128]{1,0:T(8,128)(2,1)}, u32[]{:S(2)}) copy-start(bf16[65,128]{1,0:T(8,128)(2,1)} %param.27) | copy-start | bytes 49924
  15.5 8.8 %copy-start.1 = (bf16[256,256]{1,0:T(8,128)(2,1)S(1)}, bf16[256,256]{1,0:T(8,128)(2,1)}, u32[]{:S(2)}) copy-start(bf16[256,256]{1,0:T(8,128)(2,1)} %wo_ref.1) | copy-start | bytes 393220
  28.7 34.4 %all-to-all-start.1 = ((bf16[16,8,8,256]{3,2,1,0:T(8,128)(2,1)}), bf16[16,8,8,256]{3,2,1,0:T(8,128)(2,1)S(1)}, u32[]{:S(2)}, u32[]{:S(2)}) async-start(bf16[16,8,8,256]{3,2,1,0:T(8,128)(2,1)} %bitcast.19), calls=%async_computation.1 | async-start | bytes 1048576 | tf_op jit(solution)/shard_map/all_to_all | solution.py:442
  32.8 15.3 %collective-permute-start.2 = (bf16[1,256,128]{2,1,0:T(8,128)(2,1)S(1)}, bf16[1,256,128]{2,1,0:T(8,128)(2,1)S(1)}, u32[]{:S(2)}, u32[]{:S(2)}) collective-permute-start(bf16[1,256,128]{2,1,0:T(8,128)(2,1)S(1)} %bitcast.32), channel_id=1, source_target_pairs={{0,12},{1,13},{2,14},{3,15},{4,8},{5,9},{6,10},{7,11},{8,4},{9,5},... | collective-permute-start | bytes 196616 | tf_op jit(solution)/shard_map/ppermute | solution.py:344
  36.6 17.1 %collective-permute-start.1 = (bf16[1,256,128]{2,1,0:T(8,128)(2,1)S(1)}, bf16[1,256,128]{2,1,0:T(8,128)(2,1)S(1)}, u32[]{:S(2)}, u32[]{:S(2)}) collective-permute-start(bf16[1,256,128]{2,1,0:T(8,128)(2,1)S(1)} %bitcast.33), channel_id=1, source_target_pairs={{0,8},{1,9},{2,10},{3,11},{4,12},{5,13},{6,14},{7,15},{8,0},{9,1},... | collective-permute-start | bytes 196616 | tf_op jit(solution)/shard_map/ppermute | solution.py:344
  36.6 17.1 %collective-permute-start = (bf16[1,256,128]{2,1,0:T(8,128)(2,1)S(1)}, bf16[1,256,128]{2,1,0:T(8,128)(2,1)S(1)}, u32[]{:S(2)}, u32[]{:S(2)}) collective-permute-start(bf16[1,256,128]{2,1,0:T(8,128)(2,1)S(1)} %bitcast.34), channel_id=1, source_target_pairs={{0,4},{1,5},{2,6},{3,7},{4,0},{5,1},{6,2},{7,3},{8,12},{9,13},{10,... | collective-permute-start | bytes 196616 | tf_op jit(solution)/shard_map/ppermute | solution.py:344
  53.7 7.8 %collective-permute-start.3 = (bf16[4,256,128]{2,1,0:T(8,128)(2,1)S(1)}, bf16[4,256,128]{2,1,0:T(8,128)(2,1)S(1)}, u32[]{:S(2)}, u32[]{:S(2)}) collective-permute-start(bf16[4,256,128]{2,1,0:T(8,128)(2,1)S(1)} %pad_maximum_fusion.1.refs_0_), channel_id=1, source_target_pairs={{0,2},{1,3},{2,0},{3,1},{4,6},{5,7},{6,4},{7,5},{8,10},{9,11},{10,... | collective-permute-start | bytes 786440 | tf_op jit(solution)/shard_map/ppermute | solution.py:344
  55.3 6.4 %collective-permute-start.5 = (bf16[4,256,128]{2,1,0:T(8,128)(2,1)S(1)}, bf16[4,256,128]{2,1,0:T(8,128)(2,1)S(1)}, u32[]{:S(2)}, u32[]{:S(2)}) collective-permute-start(bf16[4,256,128]{2,1,0:T(8,128)(2,1)S(1)} %pad_maximum_fusion.1.refs_0_), channel_id=1, source_target_pairs={{0,1},{1,0},{2,3},{3,2},{4,5},{5,4},{6,7},{7,6},{8,9},{9,8},{10,11... | collective-permute-start | bytes 786440 | tf_op jit(solution)/shard_map/ppermute | solution.py:344
  61.6 1.5 %collective-permute-start.4 = (bf16[4,256,128]{2,1,0:T(8,128)(2,1)S(1)}, bf16[4,256,128]{2,1,0:T(8,128)(2,1)S(1)}, u32[]{:S(2)}, u32[]{:S(2)}) collective-permute-start(bf16[4,256,128]{2,1,0:T(8,128)(2,1)S(1)} %collective-permute-done.3.refs_0_), channel_id=1, source_target_pairs={{0,1},{1,0},{2,3},{3,2},{4,5},{5,4},{6,7},{7,6},{8,9},{9,8},{10,11... | collective-permute-start | bytes 786440 | tf_op jit(solution)/shard_map/ppermute | solution.py:344

commit v2 on v1

--- a/solution.py
+++ b/solution.py
@@ -76,16 +76,18 @@
     def rows_of(ref, t):
         return take_rows(ref, pl.ds(t, seqs, stride=tokens))
 
-    normed = jnp.concatenate([rows_of(normed_ref, t) for t in range(tokens)], axis=0).astype(BF16)
-    qvg = lax.dot_general(wqvg_ref[...], normed, NT, preferred_element_type=F32)
-    keys = jnp.dot(normed, wk_ref[...], preferred_element_type=F32).astype(BF16)
-    gate = 0.5 * jnp.tanh(0.5 * (qvg[2 * channels :] + intercept_ref[...])) + 0.5
-    for t in range(tokens):
-        at = slice(t * seqs, (t + 1) * seqs)
-        queries_ref[t] = qvg[:channels, at].astype(BF16)
-        values_ref[t] = qvg[channels : 2 * channels, at].astype(BF16)
-        gate_ref[t] = gate[:, at]
-        keys_ref[t] = keys[at]
+    def project(first, count):
+        near = range(first, first + count)
+        normed = jnp.concatenate([rows_of(normed_ref, t) for t in near], axis=0).astype(BF16)
+        qvg = lax.dot_general(wqvg_ref[...], normed, NT, preferred_element_type=F32)
+        keys = jnp.dot(normed, wk_ref[...], preferred_element_type=F32).astype(BF16)
+        gate = 0.5 * jnp.tanh(0.5 * (qvg[2 * channels :] + intercept_ref[...])) + 0.5
+        for k, t in enumerate(near):
+            at = slice(k * seqs, (k + 1) * seqs)
+            queries_ref[t] = qvg[:channels, at].astype(BF16)
+            values_ref[t] = qvg[channels : 2 * channels, at].astype(BF16)
+            gate_ref[t] = gate[:, at]
+            keys_ref[t] = keys[at]
 
     groups = channels // LANES
 
@@ -131,8 +133,11 @@
                 )
                 gated_ref[t, head] = (mixed * gate_ref[t, head]).astype(BF16)
 
+    project(0, 2)
     score(0, 0)
     for t in range(tokens):
+        if t % 2 == 0 and t + 2 < tokens:
+            project(t + 2, 2)
         if t > 0:
             mix(t - 1, (t - 1) % 2)
         weigh(t % 2)
@@ -196,40 +201,27 @@
     )(x_rows, bias, flag_rows, gains, wqvg, wk, intercept, wo, wlr)
 
 
+def digit(me, stage):
+    stride, members = stage
+    return jnp.bitwise_and(me // stride, members - 1)
+
+
 def pair_kernel(
-    stages, distance, me_ref, left_ref, weight_ref, share_ref, base_ref, *refs
+    stages, me_ref, left_ref, weight_ref, share_ref, base_ref, *refs
 ):
-    (far, far_size), (near, near_size), (core, core_size) = stages
-    held_refs, refs = refs[:core_size], refs[core_size:]
-    last = distance == near_size - 1
-    if last:
-        done_refs, refs = refs[:-8], refs[-8:]
-        back_ref, out_ref, changed_ref, right_ref, outer_ref, whole_ref, pair_ref, sems = refs
-        devices, sequences = back_ref.shape[:2]
-        for d in range(devices):
-            for n in range(sequences):
-                whole_ref[n, d] = back_ref[d, n]
-        copies = [pltpu.make_async_copy(whole_ref, changed_ref, sems.at[left_ref.shape[0]])]
-        copies[0].start()
-    else:
-        done_refs, (out_ref, right_ref, outer_ref) = (), refs
+    far_stage, _, core_stage = stages
+    far_size, core_size = far_stage[1], core_stage[1]
+    held_refs, (out_ref, right_ref, outer_ref) = refs[:core_size], refs[core_size:]
     tok_local, breadth, seqs = left_ref.shape
     per_device = held_refs[0].shape[1] // breadth
-    chunk = core_size * per_device
-    width = far_size * chunk
+    width = base_ref.shape[1]
     pack = max(1, LANES // width)
     me = me_ref[0]
-    my_far = jnp.bitwise_and(me // far, far_size - 1)
-    my_near = jnp.bitwise_and(me // near, near_size - 1)
-    my_core = jnp.bitwise_and(me // core, core_size - 1)
-
-    def rows_at(f, n):
-        chip = f * near_size + jnp.bitwise_xor(my_near, n)
-        return pl.ds(pl.multiple_of(chip * chunk, chunk), chunk)
 
     for c in range(core_size):
         for f in range(far_size):
-            device = jnp.bitwise_xor(my_far, f) * core_size + jnp.bitwise_xor(my_core, c)
+            far, core = digit(me, far_stage), digit(me, core_stage)
+            device = jnp.bitwise_xor(far, f) * core_size + jnp.bitwise_xor(core, c)
             right_ref[device] = held_refs[c][f]
 
     left = left_ref[...].reshape(tok_local // pack, pack, breadth, seqs)
@@ -237,7 +229,7 @@
         [left[:, k].reshape(tok_local // pack * breadth, seqs) for k in range(pack)], axis=1
     )
     nothing = jnp.zeros((width, seqs), BF16)
-    step = 2 if breadth % 2 == 0 else 1
+    step = math.gcd(breadth, 2)
     for e in range(0, breadth, step):
         rows = []
         for k in range(e, e + step):
@@ -261,76 +253,87 @@
                 :, k * lanes : (k + 1) * lanes
             ].reshape(tok_local // pack, breadth, lanes)
 
-    share = share_ref[jnp.bitwise_xor(my_near, distance)]
     for q in range(tok_local // pack):
         projected = jnp.dot(weight_ref[...], outer_ref[q], preferred_element_type=F32)
-        projected = (projected * share[q : q + 1]).T
+        projected = (projected * share_ref[q : q + 1]).T
         for k in range(pack):
             i = q * pack + k
-            for f in range(far_size):
-                here = rows_at(f, distance)
-                mine = projected[k * width + f * chunk : k * width + (f + 1) * chunk]
-                value = (base_ref[i, here, :] + mine).astype(BF16)
-                if last:
-                    pair_ref[i, here, :] = value
-                else:
-                    out_ref[i, f * chunk : (f + 1) * chunk, :] = value
-            for n, done_ref in enumerate(done_refs):
-                for f in range(far_size):
-                    pair_ref[i, rows_at(f, n), :] = done_ref[i, f * chunk : (f + 1) * chunk, :]
-            if last:
-                copies.append(pltpu.make_async_copy(pair_ref.at[i], out_ref.at[i], sems.at[i]))
-                copies[-1].start()
-    if last:
-        for copy in copies:
-            copy.wait()
-
-
-def pair_part(distance, me, left, weight_t, share, base, held, done, back, stages):
+            mine = projected[k * width : (k + 1) * width]
+            out_ref[i] = (base_ref[i] + mine).astype(BF16)
+
+
+def pair_part(me, left, weight_t, share, base, held, stages):
     tok_local, breadth, seqs = left.shape
     pair_width = weight_t.shape[0]
     far_size, block = held[0].shape[0], held[0].shape[1:]
-    columns = base.shape[1]
-    width = columns // stages[1][1]
+    width = base.shape[1]
     pack = max(1, LANES // width)
-    size, seq_local, _, channels = back.shape
-    last = distance == stages[1][1] - 1
     vmem = pl.BlockSpec(memory_space=pltpu.VMEM)
-    scratch = [
-        pltpu.VMEM((far_size * len(held), *block), BF16),
-        pltpu.VMEM((tok_local // pack, breadth * breadth, pack * width), BF16),
-    ]
-    out_shape = jax.ShapeDtypeStruct((tok_local, width, pair_width), BF16)
-    out_specs = vmem
-    operands = [left, weight_t, share, base, *held]
-    if last:
-        operands += [*done, back]
-        out_shape = (
-            jax.ShapeDtypeStruct(base.shape, BF16),
-            jax.ShapeDtypeStruct((seq_local, size, tok_local, channels), BF16),
-        )
-        out_specs = (pl.BlockSpec(memory_space=pl.ANY), pl.BlockSpec(memory_space=pl.ANY))
-        scratch += [
-            pltpu.VMEM((seq_local, size, tok_local, channels), BF16),
-            pltpu.VMEM(base.shape, BF16),
-            pltpu.SemaphoreType.DMA((tok_local + 1,)),
-        ]
     return pl.pallas_call(
-        functools.partial(pair_kernel, stages, distance),
-        in_specs=[pl.BlockSpec(memory_space=pltpu.SMEM)] + [vmem] * len(operands),
-        out_specs=out_specs,
-        scratch_shapes=scratch,
-        out_shape=out_shape,
-        compiler_params=pltpu.CompilerParams(
-            vmem_limit_bytes=16 * 2**20 + 12 * tok_local * columns * pair_width
-        ),
+        functools.partial(pair_kernel, stages),
+        in_specs=[pl.BlockSpec(memory_space=pltpu.SMEM)] + [vmem] * (4 + len(held)),
+        out_specs=vmem,
+        scratch_shapes=[
+            pltpu.VMEM((far_size * len(held), *block), BF16),
+            pltpu.VMEM((tok_local // pack, breadth * breadth, pack * width), BF16),
+        ],
+        out_shape=jax.ShapeDtypeStruct(base.shape, BF16),
+        compiler_params=pltpu.CompilerParams(vmem_limit_bytes=24 * 2**20),
         cost_estimate=pl.CostEstimate(
             flops=2 * tok_local * width * breadth * breadth * (seqs + pair_width),
             bytes_accessed=8 * tok_local * width * pair_width,
             transcendentals=0,
         ),
         name="pair_part",
-    )(me, *operands)
+    )(me, left, weight_t, share, base, *held)
+
+
+def finish_kernel(stages, me_ref, back_ref, *refs):
+    far_stage, near_stage, _ = stages
+    near_size = near_stage[1]
+    part_refs, refs = refs[:near_size], refs[near_size:]
+    pair_out_ref, changed_out_ref, pair_ref, changed_ref, sems = refs
+    devices, sequences = back_ref.shape[:2]
+    for d in range(devices):
+        for n in range(sequences):
+            changed_ref[n, d] = back_ref[d, n]
+    copies = [pltpu.make_async_copy(changed_ref, changed_out_ref, sems.at[0])]
+    copies[0].start()
+    chunk = part_refs[0].shape[1] // far_stage[1]
+    near = digit(me_ref[0], near_stage)
+    for n in range(near_size):
+        for f in range(far_stage[1]):
+            chip = f * near_size + jnp.bitwise_xor(near, n)
+            here = pl.ds(pl.multiple_of(chip * chunk, chunk), chunk)
+            pair_ref[:, here, :] = part_refs[n][:, f * chunk : (f + 1) * chunk, :]
+    copies.append(pltpu.make_async_copy(pair_ref, pair_out_ref, sems.at[1]))
+    copies[1].start()
+    for copy in copies:
+        copy.wait()
+
+
+def finish(me, back, parts, stages):
+    size, seq_local, tok_local, channels = back.shape
+    rows, width, pair_width = parts[0].shape
+    pair_shape = (rows, width * len(parts), pair_width)
+    changed_shape = (seq_local, size, tok_local, channels)
+    vmem, anywhere = pl.BlockSpec(memory_space=pltpu.VMEM), pl.BlockSpec(memory_space=pl.ANY)
+    return pl.pallas_call(
+        functools.partial(finish_kernel, stages),
+        in_specs=[pl.BlockSpec(memory_space=pltpu.SMEM)] + [vmem] * (1 + len(parts)),
+        out_specs=(anywhere, anywhere),
+        scratch_shapes=[
+            pltpu.VMEM(pair_shape, BF16),
+            pltpu.VMEM(changed_shape, BF16),
+            pltpu.SemaphoreType.DMA((2,)),
+        ],
+        out_shape=(
+            jax.ShapeDtypeStruct(pair_shape, BF16),
+            jax.ShapeDtypeStruct(changed_shape, BF16),
+        ),
+        compiler_params=pltpu.CompilerParams(vmem_limit_bytes=24 * 2**20),
+        name="finish",
+    )(me, back, *parts)
 
 
 def gather_stages(size):
@@ -344,17 +347,13 @@
     return lax.ppermute(held, "wide", [(d, d ^ distance) for d in range(size)])
 
 
-def gather_blocks(block, size, stages):
-    (far, far_size), (near, near_size), (core, core_size) = stages
+def gather_column(block, size, stages):
+    (far, far_size), _, (core, core_size) = stages
     block = block[None]
     column = jnp.concatenate(
         [block] + [exchange(block, size, f * far) for f in range(1, far_size)], axis=0
     )
-    held = []
-    for n in range(near_size):
-        here = exchange(column, size, n * near) if n else column
-        held.append([here] + [exchange(here, size, c * core) for c in range(1, core_size)])
-    return held
+    return [column] + [exchange(column, size, c * core) for c in range(1, core_size)]
 
 
 def on_device(
@@ -383,7 +382,8 @@
     stages = gather_stages(size)
 
     sent = homolog_stack_state.reshape(seq_local, size, tok_local, channels).transpose(1, 0, 2, 3)
-    x_rows = lax.all_to_all(sent, "wide", 0, 0, tiled=True).reshape(seqs * tok_local, channels)
+    x_rows = lax.all_to_all(sent, "wide", 0, 0, tiled=True)
+    x_rows = x_rows.reshape(seqs * tok_local, channels)
 
     flags = present_flags.astype(F32)
     mine = lax.dynamic_slice_in_dim(flags, me * tok_local, tok_local, 1)
@@ -402,27 +402,47 @@
         .transpose(2, 1, 0)
         .reshape(pair_width, breadth * breadth)
     )
-    counts = jnp.dot(mine.T, flags, precision=lax.Precision.HIGHEST)
-    far_size, near_size = stages[0][1], stages[1][1]
-    pack = max(1, LANES * near_size // columns)
-    share = (1.0 / counts).reshape(tok_local, far_size, near_size, -1).transpose(2, 0, 1, 3)
-    share = share.reshape(near_size, tok_local // pack, pack * columns // near_size)
-    labels_mine = lax.dynamic_slice_in_dim(chain_ordinal_labels, me * tok_local, tok_local, 0)
-    offsets = (
-        jnp.clip(labels_mine[:, None] - chain_ordinal_labels[None, :], -RELPOS_CLIP, RELPOS_CLIP)
-        + RELPOS_CLIP
-    )
+    (_, far_size), (near, near_size), (_, core_size) = stages
+    my_near = digit(me, stages[1])
+    chunk = core_size * tok_local
+    width = far_size * chunk
+    pack = max(1, LANES // width)
+
+    def near_columns(values, axis, near_digit):
+        shape = values.shape
+        split = values.reshape(shape[:axis] + (far_size, near_size, chunk) + shape[axis + 1 :])
+        taken = lax.dynamic_index_in_dim(split, near_digit, axis + 1, keepdims=False)
+        return taken.reshape(shape[:axis] + (width,) + shape[axis + 1 :])
+
+    flags_here = near_columns(flags, 1, my_near)
+    labels_here = near_columns(chain_ordinal_labels, 0, my_near)
     span = clipped_separation_embedding.shape[0]
-    one_hot = (offsets[:, :, None] == jnp.arange(span, dtype=jnp.int32)[None, None, :]).astype(BF16)
-    relpos = jnp.dot(
-        one_hot.reshape(tok_local * columns, span),
-        clipped_separation_embedding,
-        preferred_element_type=F32,
-    ).reshape(tok_local, columns, pair_width)
-    base = pairwise_repr.astype(F32) + relpos
-
-    x_rows, base, share, projection_t = lax.optimization_barrier(
-        (x_rows, base, share, projection_t)
+    shares, bases = [], []
+    for n in range(near_size):
+        first = jnp.bitwise_xor(me, n * near) * tok_local
+        rows_flags = lax.dynamic_slice_in_dim(flags, first, tok_local, 1)
+        counts = jnp.dot(rows_flags.T, flags_here, precision=lax.Precision.HIGHEST)
+        shares.append((1.0 / counts).reshape(tok_local // pack, pack * width))
+        labels = lax.dynamic_slice_in_dim(chain_ordinal_labels, first, tok_local, 0)
+        offsets = (
+            jnp.clip(labels[:, None] - labels_here[None, :], -RELPOS_CLIP, RELPOS_CLIP)
+            + RELPOS_CLIP
+        )
+        one_hot = (offsets[:, :, None] == jnp.arange(span, dtype=jnp.int32)[None, None, :]).astype(
+            BF16
+        )
+        relpos = jnp.dot(
+            one_hot.reshape(tok_local * width, span),
+            clipped_separation_embedding,
+            preferred_element_type=F32,
+        ).reshape(tok_local, width, pair_width)
+        entries = near_columns(pairwise_repr, 1, jnp.bitwise_xor(my_near, n))
+        if n:
+            entries = exchange(entries, size, n * near)
+        bases.append(entries.astype(F32) + relpos)
+
+    x_rows, bases, shares, projection_t = lax.optimization_barrier(
+        (x_rows, bases, shares, projection_t)
     )
 
     changed_rows, left, right = attention(
@@ -438,26 +458,17 @@
         tok_local,
     )
 
-    right_held = gather_blocks(right, size, stages)
+    me = me.reshape(1)
+    held = gather_column(right, size, stages)
     back = lax.all_to_all(
         changed_rows.reshape(size, seq_local, tok_local, channels), "wide", 0, 0, tiled=True
     )
-    done = []
-    for distance, held in enumerate(right_held):
-        part = pair_part(
-            distance,
-            me.reshape(1),
-            left,
-            projection_t,
-            share,
-            base,
-            held,
-            done[:],
-            back,
-            stages,
-        )
-        done.append(part)
-    couple_state_changed, homolog_changed = done[-1]
+    lefts = [left] + [exchange(left, size, n * near) for n in range(1, near_size)]
+    parts = []
+    for n in range(near_size):
+        part = pair_part(me, lefts[n], projection_t, shares[n], bases[n], held, stages)
+        parts.append(exchange(part, size, n * near) if n else part)
+    couple_state_changed, homolog_changed = finish(me, back, parts, stages)
     return (homolog_changed.reshape(seq_local, columns, channels), couple_state_changed)
 
 

time: 65.7 us -> 66.7 us (1.015)
  starting transfers between devices: 17.7 us -> 19.9 us
  waiting for transfers between devices: 31.3 us -> 30.1 us
    ppermute x6 -> x7, starting transfers between devices: 5.99 us -> 10.6 us  [exchange(): return lax.ppermute(held, 'wide', [(d, d ^ distance) for d in range(size)])]
    all_to_all x1, starting transfers between devices: 7.55 us -> 5.11 us  [on_device(): x_rows = lax.all_to_all(sent, 'wide', 0, 0, tiled=True)]
    unnamed x32 -> x30, local copies, waits for them, and re-layouts: 5.44 us -> 3.81 us
    ppermute x6 -> x7, waiting for transfers between devices: 22.8 us -> 21.5 us  [exchange(): return lax.ppermute(held, 'wide', [(d, d ^ distance) for d in range(size)])]
    dynamic_slice x1 -> x4, local copies, waits for them, and re-layouts: 0.07 us -> 1.15 us  [the longest x3 1.07 us: near_columns(): lax.dynamic_index_in_dim(split, near_digit, axis + 1, keepdims=False)]
    pallas_call x2 -> x3, Pallas kernels: 3.39 us -> 3.49 us  [the longest x2 2.53 us: pair_part(): pl.pallas_call(functools.partial(pair_kernel, stages), in_specs=[pl.Block...]
  transfers between devices with their start and end apart: 8 -> 9, of which waited for: 5 -> 5; matrix products, arithmetic and copies ran while one was open for 3% -> 5% of each run, Pallas kernels for 2% -> 4%
where the time goes in v2:
time: 66.7 us; the launch traced here: 66.2 us
  waiting for transfers between devices  30.1 us (45%)
  starting transfers between devices  19.9 us (30%)
  Pallas kernels  7.71 us (12%)
  local copies, waits for them, and re-layouts  6.55 us (10%)
  between operations  0.89 us (1%)
  matrix products  0.82 us (1%)
    ppermute x7, waiting for transfers between devices, exchange(): return lax.ppermute(held, 'wide', [(d, d ^ distance) for d in range(size)])  21.5 us
    ppermute x7, starting transfers between devices, exchange(): return lax.ppermute(held, 'wide', [(d, d ^ distance) for d in range(size)])  10.6 us
    all_to_all x1, waiting for transfers between devices, on_device(): x_rows = lax.all_to_all(sent, 'wide', 0, 0, tiled=True)  8.61 us
    all_to_all x1, starting transfers between devices, on_device(): x_rows = lax.all_to_all(sent, 'wide', 0, 0, tiled=True)  5.11 us
    pallas_call x1, Pallas kernels, attention(): pl.pallas_call(functools.partial(attention_kernel, tokens), out_shape=(ja...  4.22 us
    all_to_all x1, starting transfers between devices, on_device(): lax.all_to_all(changed_rows.reshape(size, seq_local, tok_local, channels)...  4.17 us
    unnamed x30, local copies, waits for them, and re-layouts  3.81 us
    pallas_call x2, Pallas kernels, pair_part(): pl.pallas_call(functools.partial(pair_kernel, stages), in_specs=[pl.Block...  2.53 us
  transfers between devices with their start and end apart: 9, of which 5 were waited for; matrix products, arithmetic and copies ran while one was open for 5% of the time, Pallas kernels for 4%

profile of v2, /device:TPU:0, one launch (start us, length us, event | category | flops | bytes accessed | tf_op | source)
XLA Modules:
  0.0 66.2 jit_solution(17229895505292813739)
XLA Ops:
  0.6 0.0 copy-start
  0.7 1.0 %constant_dynamic-slice_fusion.2 = (bf16[8,4,1,16,128]{4,3,2,1,0:T(8,128)(2,1)S(1)}, bf16[8,4,1,16,128]{4,3,2,1,0:T(8,128)(2,1)S(1)}) fusion(bf16[8,4,2,16,128]{4,3,2,1,0:T(8,128)(2,1)} %bitcast.54, s32[]{:T(128)S(6)} %select_n.28, s32[]{:T(128)S(6)} %select_n.26), kind=kLoop, calls=%fused_computation.24 | loop fusion | bytes 524296 | tf_op jit(solution)/shard_map/jit(dynamic_index_in_dim)/dynamic_slice | solution.py:414
  1.7 3.1 %collective-permute-start = (bf16[8,64,128]{2,1,0:T(8,128)(2,1)S(1)}, bf16[8,64,128]{2,1,0:T(8,128)(2,1)S(1)}, u32[]{:S(2)}, u32[]{:S(2)}) collective-permute-start(bf16[8,64,128]{2,1,0:T(8,128)(2,1)S(1)} %bitcast.57), channel_id=1, source_target_pairs={{0,2},{1,3},{2,0},{3,1},{4,6},{5,7},{6,4},{7,5},{8,10},{9,11},{10,... | collective-permute-start | bytes 393224 | tf_op jit(solution)/shard_map/ppermute | solution.py:347
  4.8 0.8 %copy_bitcast_fusion = bf16[16,8,8,256]{3,2,1,0:T(8,128)(2,1)} fusion(bf16[8,128,256]{2,1,0:T(8,128)(2,1)S(1)} %copy-done), kind=kLoop, calls=%fused_computation.3 | loop fusion | bytes 1048576 | tf_op jit(solution)/shard_map/transpose | solution.py:384
  5.6 5.1 %all-to-all-start = ((bf16[16,8,8,256]{3,2,1,0:T(8,128)(2,1)}), bf16[16,8,8,256]{3,2,1,0:T(8,128)(2,1)S(1)}, u32[]{:S(2)}, u32[]{:S(2)}) async-start(bf16[16,8,8,256]{3,2,1,0:T(8,128)(2,1)} %copy_bitcast_fusion), calls=%async_computation | async-start | bytes 1048576 | tf_op jit(solution)/shard_map/all_to_all | solution.py:385
  10.7 0.0 copy-start.2
  10.8 0.1 reshape.147
  10.9 0.1 sub.44
  11.0 0.1 copy.37
  11.1 0.1 fusion.8
  11.2 0.1 convolution_divide_fusion
  11.3 0.2 convolution_divide_fusion.1
  11.5 0.1 clamp_add_fusion
  11.6 0.5 copy-done.8
  12.1 0.2 copy-done.7
  12.3 0.2 copy.39
  12.4 0.0 copy-start.5
  12.5 0.7 %copy-done.5 = bf16[65,128]{1,0:T(8,128)(2,1)S(1)} copy-done((bf16[65,128]{1,0:T(8,128)(2,1)S(1)}, bf16[65,128]{1,0:T(8,128)(2,1)}, u32[]{:S(2)}) %copy-start.5) | copy-done | bytes 16664
  13.2 0.3 convolution_add_fusion.base_ref
  13.4 0.0 copy-start.11
  13.4 0.4 copy-done.12
  13.9 0.3 copy-done.11
  14.2 0.1 copy.47
  14.3 0.1 reshape.151.share_ref
  14.4 0.1 reshape.152.share_ref
  14.4 0.6 copy-done.4
  15.0 0.1 copy.40
  15.1 0.0 copy-start.10
  15.1 0.7 %copy-done.10 = f32[256]{0:T(256)S(1)} copy-done((f32[256]{0:T(256)S(1)}, f32[256]{0:T(256)}, u32[]{:S(2)}) %copy-start.10) | copy-done | bytes 1048
  15.8 0.1 copy.42.intercept_ref
  16.0 0.1 copy.38
  16.2 0.3 convert_add_fusion.base_ref
  16.4 8.6 %all-to-all-done = bf16[16,8,8,256]{3,2,1,0:T(8,128)(2,1)S(1)} async-done(((bf16[16,8,8,256]{3,2,1,0:T(8,128)(2,1)}), bf16[16,8,8,256]{3,2,1,0:T(8,128)(2,1)S(1)}, u32[]{:S(2)}, u32[]{:S(2)}) %all-to-all-start) | async-done | bytes 524320 | tf_op jit(solution)/shard_map/all_to_all | solution.py:385
  25.0 4.2 %attention.1 = (bf16[1024,256]{1,0:T(8,128)(2,1)}, bf16[8,32,128]{2,1,0:T(8,128)(2,1)S(1)}, bf16[256,128]{1,0:T(8,128)(2,1)S(1)}) custom-call(bf16[1024,256]{1,0:T(8,128)(2,1)S(1)} %bitcast.42, bf16[128,128]{1,0:T(8,128)(2,1)S(1)} %pad.5.clone.bias_ref, f32[8,1,128]{2,1,0:T(1,128)S(1)} %bitcast.47, f32[2,256]{1,0:T(2,128)S(1)} %pad_maximum_fusion.3.gains_ref, ...), custom_call_target="tpu_custom_call" | custom-call | flops 805306368 | bytes 1048576 | tf_op jit(solution)/shard_map/attention/pallas_call | solution.py:169
  29.2 4.2 %all-to-all-start.1 = ((bf16[16,8,8,256]{3,2,1,0:T(8,128)(2,1)}), bf16[16,8,8,256]{3,2,1,0:T(8,128)(2,1)S(1)}, u32[]{:S(2)}, u32[]{:S(2)}) async-start(bf16[16,8,8,256]{3,2,1,0:T(8,128)(2,1)} %bitcast.22), calls=%async_computation.1 | async-start | bytes 1048576 | tf_op jit(solution)/shard_map/all_to_all | solution.py:463
  33.4 3.7 %collective-permute-start.3 = (bf16[1,256,128]{2,1,0:T(8,128)(2,1)S(1)}, bf16[1,256,128]{2,1,0:T(8,128)(2,1)S(1)}, u32[]{:S(2)}, u32[]{:S(2)}) collective-permute-start(bf16[1,256,128]{2,1,0:T(8,128)(2,1)S(1)} %bitcast.43), channel_id=1, source_target_pairs={{0,12},{1,13},{2,14},{3,15},{4,8},{5,9},{6,10},{7,11},{8,4},{9,5},... | collective-permute-start | bytes 196616 | tf_op jit(solution)/shard_map/ppermute | solution.py:347
  37.2 0.7 %collective-permute-start.1 = (bf16[1,256,128]{2,1,0:T(8,128)(2,1)S(1)}, bf16[1,256,128]{2,1,0:T(8,128)(2,1)S(1)}, u32[]{:S(2)}, u32[]{:S(2)}) collective-permute-start(bf16[1,256,128]{2,1,0:T(8,128)(2,1)S(1)} %bitcast.45), channel_id=1, source_target_pairs={{0,4},{1,5},{2,6},{3,7},{4,0},{5,1},{6,2},{7,3},{8,12},{9,13},{10,... | collective-permute-start | bytes 196616 | tf_op jit(solution)/shard_map/ppermute | solution.py:347
  37.9 10.9 %collective-permute-done.3 = bf16[1,256,128]{2,1,0:T(8,128)(2,1)S(1)} collective-permute-done((bf16[1,256,128]{2,1,0:T(8,128)(2,1)S(1)}, bf16[1,256,128]{2,1,0:T(8,128)(2,1)S(1)}, u32[]{:S(2)}, u32[]{:S(2)}) %collective-permute-start.3) | collective-permute-done | bytes 65568 | tf_op jit(solution)/shard_map/ppermute | solution.py:347
  48.8 5.5 %collective-permute-done.2 = bf16[1,256,128]{2,1,0:T(8,128)(2,1)S(1)} collective-permute-done((bf16[1,256,128]{2,1,0:T(8,128)(2,1)S(1)}, bf16[1,256,128]{2,1,0:T(8,128)(2,1)S(1)}, u32[]{:S(2)}, u32[]{:S(2)}) %collective-permute-start.2) | collective-permute-done | bytes 65568 | tf_op jit(solution)/shard_map/ppermute | solution.py:347
  54.3 0.1 collective-permute-start.4
  54.4 1.5 %collective-permute-start.5 = (bf16[8,32,128]{2,1,0:T(8,128)(2,1)S(1)}, bf16[8,32,128]{2,1,0:T(8,128)(2,1)S(1)}, u32[]{:S(2)}, u32[]{:S(2)}) collective-permute-start(bf16[8,32,128]{2,1,0:T(8,128)(2,1)S(1)} %get-tuple-element.15.left_ref), channel_id=1, source_target_pairs={{0,2},{1,3},{2,0},{3,1},{4,6},{5,7},{6,4},{7,5},{8,10},{9,11},{10,... | collective-permute-start | bytes 196616 | tf_op jit(solution)/shard_map/ppermute | solution.py:347
  55.9 0.1 copy.43.weight_ref
  56.1 2.8 %collective-permute-done.5.left_ref = bf16[8,32,128]{2,1,0:T(8,128)(2,1)S(1)} collective-permute-done((bf16[8,32,128]{2,1,0:T(8,128)(2,1)S(1)}, bf16[8,32,128]{2,1,0:T(8,128)(2,1)S(1)}, u32[]{:S(2)}, u32[]{:S(2)}) %collective-permute-start.5) | collective-permute-done | bytes 65568 | tf_op jit(solution)/shard_map/ppermute | solution.py:347
  58.9 1.3 %pair_part.3 = bf16[8,64,128]{2,1,0:T(8,128)(2,1)S(1)} custom-call(s32[1]{0:T(128)} %bitcast.me_ref, bf16[8,32,128]{2,1,0:T(8,128)(2,1)S(1)} %collective-permute-done.5.left_ref, bf16[128,1024]{1,0:T(8,128)(2,1)S(1)} %copy.43.weight_ref, f32[4,128]{1,0:T(4,128)S(1)} %reshape.152.share_ref, f32[8,64,128]{2,1,0:T(8,128)S(1)} %convert_add_fusion.base_ref, ...), custom_call_target="tpu_custom_call" | custom-call | flops 268435456 | bytes 524288 | tf_op jit(solution)/shard_map/pair_part/pallas_call | solution.py:272
  60.2 1.5 %collective-permute-start.6 = (bf16[8,64,128]{2,1,0:T(8,128)(2,1)S(1)}, bf16[8,64,128]{2,1,0:T(8,128)(2,1)S(1)}, u32[]{:S(2)}, u32[]{:S(2)}) collective-permute-start(bf16[8,64,128]{2,1,0:T(8,128)(2,1)S(1)} %pair_part.3), channel_id=1, source_target_pairs={{0,2},{1,3},{2,0},{3,1},{4,6},{5,7},{6,4},{7,5},{8,10},{9,11},{10,... | collective-permute-start | bytes 393224 | tf_op jit(solution)/shard_map/ppermute | solution.py:347
  61.7 1.3 %pair_part.2.refs_0_ = bf16[8,64,128]{2,1,0:T(8,128)(2,1)S(1)} custom-call(s32[1]{0:T(128)} %bitcast.me_ref, bf16[8,32,128]{2,1,0:T(8,128)(2,1)S(1)} %get-tuple-element.15.left_ref, bf16[128,1024]{1,0:T(8,128)(2,1)S(1)} %copy.43.weight_ref, f32[4,128]{1,0:T(4,128)S(1)} %reshape.151.share_ref, f32[8,64,128]{2,1,0:T(8,128)S(1)} %convolution_add_fusion.base_ref, ...), custom_call_target="tpu_custom_call" | custom-call | flops 268435456 | bytes 524288 | tf_op jit(solution)/shard_map/pair_part/pallas_call | solution.py:272
  63.0 2.2 %collective-permute-done.6.refs_1_ = bf16[8,64,128]{2,1,0:T(8,128)(2,1)S(1)} collective-permute-done((bf16[8,64,128]{2,1,0:T(8,128)(2,1)S(1)}, bf16[8,64,128]{2,1,0:T(8,128)(2,1)S(1)}, u32[]{:S(2)}, u32[]{:S(2)}) %collective-permute-start.6) | collective-permute-done | bytes 131104 | tf_op jit(solution)/shard_map/ppermute | solution.py:347
  65.2 1.0 %finish.1 = (bf16[8,128,128]{2,1,0:T(8,128)(2,1)}, bf16[8,16,8,256]{3,2,1,0:T(8,128)(2,1)}) custom-call(s32[1]{0:T(128)} %bitcast.me_ref, bf16[16,8,8,256]{3,2,1,0:T(8,128)(2,1)S(1)} %all-to-all-done.1.back_ref, bf16[8,64,128]{2,1,0:T(8,128)(2,1)S(1)} %pair_part.2.refs_0_, bf16[8,64,128]{2,1,0:T(8,128)(2,1)S(1)} %collective-permute-done.6.refs_1_), custom_call_target="tpu_custom_call" | custom-call | tf_op jit(solution)/shard_map/finish/pallas_call | solution.py:321
  (30 shorter events, 0.2 us)
Async XLA Ops:
  0.6 4.1 %copy-start = (bf16[8,128,256]{2,1,0:T(8,128)(2,1)S(1)}, bf16[8,128,256]{2,1,0:T(8,128)(2,1)}, u32[]{:S(2)}) copy-start(bf16[8,128,256]{2,1,0:T(8,128)(2,1)} %param.14) | copy-start | bytes 1572868
  1.7 14.4 %collective-permute-start = (bf16[8,64,128]{2,1,0:T(8,128)(2,1)S(1)}, bf16[8,64,128]{2,1,0:T(8,128)(2,1)S(1)}, u32[]{:S(2)}, u32[]{:S(2)}) collective-permute-start(bf16[8,64,128]{2,1,0:T(8,128)(2,1)S(1)} %bitcast.57), channel_id=1, source_target_pairs={{0,2},{1,3},{2,0},{3,1},{4,6},{5,7},{6,4},{7,5},{8,10},{9,11},{10,... | collective-permute-start | bytes 393224 | tf_op jit(solution)/shard_map/ppermute | solution.py:347
  5.6 5.1 %copy-start.9 = (s32[128]{0:T(128)S(1)}, s32[128]{0:T(128)}, u32[]{:S(2)}) copy-start(s32[128]{0:T(128)} %param.16) | copy-start | bytes 1540
  5.6 5.3 %copy-start.6 = (s32[128,128]{1,0:T(8,128)S(1)}, s32[128,128]{1,0:T(8,128)}, u32[]{:S(2)}) copy-start(s32[128,128]{1,0:T(8,128)} %param.15) | copy-start | bytes 196612
  5.6 19.4 %all-to-all-start = ((bf16[16,8,8,256]{3,2,1,0:T(8,128)(2,1)}), bf16[16,8,8,256]{3,2,1,0:T(8,128)(2,1)S(1)}, u32[]{:S(2)}, u32[]{:S(2)}) async-start(bf16[16,8,8,256]{3,2,1,0:T(8,128)(2,1)} %copy_bitcast_fusion), calls=%async_computation | async-start | bytes 1048576 | tf_op jit(solution)/shard_map/all_to_all | solution.py:385
  10.7 1.5 %copy-start.2 = (bf16[256,768]{1,0:T(8,128)(2,1)S(1)}, bf16[256,768]{1,0:T(8,128)(2,1)}, u32[]{:S(2)}) copy-start(bf16[256,768]{1,0:T(8,128)(2,1)} %param.19) | copy-start | bytes 1179652
  11.3 0.8 %copy-start.8 = (bf16[256,32]{0,1:T(8,128)(2,1)S(1)}, bf16[256,32]{0,1:T(8,128)(2,1)}, u32[]{:S(2)}) copy-start(bf16[256,32]{0,1:T(8,128)(2,1)} %param.24) | copy-start | bytes 49156
  11.5 0.8 %copy-start.7 = (bf16[256,32]{0,1:T(8,128)(2,1)S(1)}, bf16[256,32]{0,1:T(8,128)(2,1)}, u32[]{:S(2)}) copy-start(bf16[256,32]{0,1:T(8,128)(2,1)} %param.25) | copy-start | bytes 49156
  12.4 0.7 %copy-start.5 = (bf16[65,128]{1,0:T(8,128)(2,1)S(1)}, bf16[65,128]{1,0:T(8,128)(2,1)}, u32[]{:S(2)}) copy-start(bf16[65,128]{1,0:T(8,128)(2,1)} %param.27) | copy-start | bytes 49924
  13.2 0.7 %copy-start.12 = (f32[256]{0:T(256)S(1)}, f32[256]{0:T(256)}, u32[]{:S(2)}) copy-start(f32[256]{0:T(256)} %param.18) | copy-start | bytes 3076
  13.4 0.7 %copy-start.11 = (f32[256]{0:T(256)S(1)}, f32[256]{0:T(256)}, u32[]{:S(2)}) copy-start(f32[256]{0:T(256)} %param.23) | copy-start | bytes 3076
  14.1 0.9 %copy-start.4 = (bf16[256,256]{1,0:T(8,128)(2,1)S(1)}, bf16[256,256]{1,0:T(8,128)(2,1)}, u32[]{:S(2)}) copy-start(bf16[256,256]{1,0:T(8,128)(2,1)} %param.20) | copy-start | bytes 393220
  14.1 1.8 %copy-start.3 = (bf16[1024,128]{1,0:T(8,128)(2,1)S(1)}, bf16[1024,128]{1,0:T(8,128)(2,1)}, u32[]{:S(2)}) copy-start(bf16[1024,128]{1,0:T(8,128)(2,1)} %param.26) | copy-start | bytes 786436
  15.1 0.7 %copy-start.10 = (f32[256]{0:T(256)S(1)}, f32[256]{0:T(256)}, u32[]{:S(2)}) copy-start(f32[256]{0:T(256)} %param.21) | copy-start | bytes 3076
  16.1 8.9 %copy-start.1 = (bf16[256,256]{1,0:T(8,128)(2,1)S(1)}, bf16[256,256]{1,0:T(8,128)(2,1)}, u32[]{:S(2)}) copy-start(bf16[256,256]{1,0:T(8,128)(2,1)} %wo_ref.1) | copy-start | bytes 393220
  29.2 36.0 %all-to-all-start.1 = ((bf16[16,8,8,256]{3,2,1,0:T(8,128)(2,1)}), bf16[16,8,8,256]{3,2,1,0:T(8,128)(2,1)S(1)}, u32[]{:S(2)}, u32[]{:S(2)}) async-start(bf16[16,8,8,256]{3,2,1,0:T(8,128)(2,1)} %bitcast.22), calls=%async_computation.1 | async-start | bytes 1048576 | tf_op jit(solution)/shard_map/all_to_all | solution.py:463
  33.4 15.3 %collective-permute-start.3 = (bf16[1,256,128]{2,1,0:T(8,128)(2,1)S(1)}, bf16[1,256,128]{2,1,0:T(8,128)(2,1)S(1)}, u32[]{:S(2)}, u32[]{:S(2)}) collective-permute-start(bf16[1,256,128]{2,1,0:T(8,128)(2,1)S(1)} %bitcast.43), channel_id=1, source_target_pairs={{0,12},{1,13},{2,14},{3,15},{4,8},{5,9},{6,10},{7,11},{8,4},{9,5},... | collective-permute-start | bytes 196616 | tf_op jit(solution)/shard_map/ppermute | solution.py:347
  37.2 17.1 %collective-permute-start.2 = (bf16[1,256,128]{2,1,0:T(8,128)(2,1)S(1)}, bf16[1,256,128]{2,1,0:T(8,128)(2,1)S(1)}, u32[]{:S(2)}, u32[]{:S(2)}) collective-permute-start(bf16[1,256,128]{2,1,0:T(8,128)(2,1)S(1)} %bitcast.44), channel_id=1, source_target_pairs={{0,8},{1,9},{2,10},{3,11},{4,12},{5,13},{6,14},{7,15},{8,0},{9,1},... | collective-permute-start | bytes 196616 | tf_op jit(solution)/shard_map/ppermute | solution.py:347
  37.2 17.1 %collective-permute-start.1 = (bf16[1,256,128]{2,1,0:T(8,128)(2,1)S(1)}, bf16[1,256,128]{2,1,0:T(8,128)(2,1)S(1)}, u32[]{:S(2)}, u32[]{:S(2)}) collective-permute-start(bf16[1,256,128]{2,1,0:T(8,128)(2,1)S(1)} %bitcast.45), channel_id=1, source_target_pairs={{0,4},{1,5},{2,6},{3,7},{4,0},{5,1},{6,2},{7,3},{8,12},{9,13},{10,... | collective-permute-start | bytes 196616 | tf_op jit(solution)/shard_map/ppermute | solution.py:347
  54.3 4.6 %collective-permute-start.4 = (bf16[4,256,128]{2,1,0:T(8,128)(2,1)S(1)}, bf16[4,256,128]{2,1,0:T(8,128)(2,1)S(1)}, u32[]{:S(2)}, u32[]{:S(2)}) collective-permute-start(bf16[4,256,128]{2,1,0:T(8,128)(2,1)S(1)} %pad_maximum_fusion.1.refs_0_), channel_id=1, source_target_pairs={{0,1},{1,0},{2,3},{3,2},{4,5},{5,4},{6,7},{7,6},{8,9},{9,8},{10,11... | collective-permute-start | bytes 786440 | tf_op jit(solution)/shard_map/ppermute | solution.py:347
  54.4 4.5 %collective-permute-start.5 = (bf16[8,32,128]{2,1,0:T(8,128)(2,1)S(1)}, bf16[8,32,128]{2,1,0:T(8,128)(2,1)S(1)}, u32[]{:S(2)}, u32[]{:S(2)}) collective-permute-start(bf16[8,32,128]{2,1,0:T(8,128)(2,1)S(1)} %get-tuple-element.15.left_ref), channel_id=1, source_target_pairs={{0,2},{1,3},{2,0},{3,1},{4,6},{5,7},{6,4},{7,5},{8,10},{9,11},{10,... | collective-permute-start | bytes 196616 | tf_op jit(solution)/shard_map/ppermute | solution.py:347
  60.2 5.0 %collective-permute-start.6 = (bf16[8,64,128]{2,1,0:T(8,128)(2,1)S(1)}, bf16[8,64,128]{2,1,0:T(8,128)(2,1)S(1)}, u32[]{:S(2)}, u32[]{:S(2)}) collective-permute-start(bf16[8,64,128]{2,1,0:T(8,128)(2,1)S(1)} %pair_part.3), channel_id=1, source_target_pairs={{0,2},{1,3},{2,0},{3,1},{4,6},{5,7},{6,4},{7,5},{8,10},{9,11},{10,... | collective-permute-start | bytes 393224 | tf_op jit(solution)/shard_map/ppermute | solution.py:347

commit v3 on v2

--- a/solution.py
+++ b/solution.py
@@ -84,7 +84,7 @@
         gate = 0.5 * jnp.tanh(0.5 * (qvg[2 * channels :] + intercept_ref[...])) + 0.5
         for k, t in enumerate(near):
             at = slice(k * seqs, (k + 1) * seqs)
-            queries_ref[t] = qvg[:channels, at].astype(BF16)
+            queries_ref[t] = (qvg[:channels, at] * scale).astype(BF16)
             values_ref[t] = qvg[channels : 2 * channels, at].astype(BF16)
             gate_ref[t] = gate[:, at]
             keys_ref[t] = keys[at]
@@ -118,7 +118,7 @@
                 head = slice(h * seqs, (h + 1) * seqs)
                 logits = logits_refs[held][g, :, head]
                 highest = jnp.max(logits, axis=0, keepdims=True)
-                powers = jnp.exp2((logits - highest) * scale)
+                powers = jnp.exp2(logits - highest)
                 share = 1.0 / jnp.sum(powers, axis=0, keepdims=True)
                 weights_refs[held][g, :, head] = (powers * share).astype(BF16)
 
@@ -388,7 +388,7 @@
     flags = present_flags.astype(F32)
     mine = lax.dynamic_slice_in_dim(flags, me * tok_local, tok_local, 1)
     flag_rows = mine.T[:, None, :]
-    masks = (1000000000.0 * math.sqrt(HEAD_SIZE)) * (mine - 1.0)
+    masks = (1000000000.0 * math.log2(math.e)) * (mine - 1.0)
     bias = jnp.pad(masks, ((0, 0), (0, LANES - tok_local))).astype(BF16)
     gains = jnp.stack([heeding_normalizer_gains, dyadic_normalizer_gains])
     weights_t = retrieval_weights_qkv.T

time: 66.7 us -> 66.7 us (level)
  no operation moved by 1% of the time
where the time goes in v3:
time: 66.7 us; the launch traced here: 66.1 us
  waiting for transfers between devices  30.1 us (45%)
  starting transfers between devices  19.9 us (30%)
  Pallas kernels  7.67 us (11%)
  local copies, waits for them, and re-layouts  6.55 us (10%)
  between operations  0.89 us (1%)
  matrix products  0.82 us (1%)
    ppermute x7, waiting for transfers between devices, exchange(): return lax.ppermute(held, 'wide', [(d, d ^ distance) for d in range(size)])  21.5 us
    ppermute x7, starting transfers between devices, exchange(): return lax.ppermute(held, 'wide', [(d, d ^ distance) for d in range(size)])  10.6 us
    all_to_all x1, waiting for transfers between devices, on_device(): x_rows = lax.all_to_all(sent, 'wide', 0, 0, tiled=True)  8.61 us
    all_to_all x1, starting transfers between devices, on_device(): x_rows = lax.all_to_all(sent, 'wide', 0, 0, tiled=True)  5.11 us
    pallas_call x1, Pallas kernels, attention(): pl.pallas_call(functools.partial(attention_kernel, tokens), out_shape=(ja...  4.18 us
    all_to_all x1, starting transfers between devices, on_device(): lax.all_to_all(changed_rows.reshape(size, seq_local, tok_local, channels)...  4.16 us
    unnamed x30, local copies, waits for them, and re-layouts  3.81 us
    pallas_call x2, Pallas kernels, pair_part(): pl.pallas_call(functools.partial(pair_kernel, stages), in_specs=[pl.Block...  2.54 us
  transfers between devices with their start and end apart: 9, of which 5 were waited for; matrix products, arithmetic and copies ran while one was open for 5% of the time, Pallas kernels for 4%

profile of v3, /device:TPU:0, one launch (start us, length us, event | category | flops | bytes accessed | tf_op | source)
XLA Modules:
  0.0 66.1 jit_solution(16289822311298075302)
XLA Ops:
  0.6 0.0 copy-start
  0.7 1.0 %constant_dynamic-slice_fusion.2 = (bf16[8,4,1,16,128]{4,3,2,1,0:T(8,128)(2,1)S(1)}, bf16[8,4,1,16,128]{4,3,2,1,0:T(8,128)(2,1)S(1)}) fusion(bf16[8,4,2,16,128]{4,3,2,1,0:T(8,128)(2,1)} %bitcast.54, s32[]{:T(128)S(6)} %select_n.28, s32[]{:T(128)S(6)} %select_n.26), kind=kLoop, calls=%fused_computation.24 | loop fusion | bytes 524296 | tf_op jit(solution)/shard_map/jit(dynamic_index_in_dim)/dynamic_slice | solution.py:414
  1.7 3.1 %collective-permute-start = (bf16[8,64,128]{2,1,0:T(8,128)(2,1)S(1)}, bf16[8,64,128]{2,1,0:T(8,128)(2,1)S(1)}, u32[]{:S(2)}, u32[]{:S(2)}) collective-permute-start(bf16[8,64,128]{2,1,0:T(8,128)(2,1)S(1)} %bitcast.57), channel_id=1, source_target_pairs={{0,2},{1,3},{2,0},{3,1},{4,6},{5,7},{6,4},{7,5},{8,10},{9,11},{10,... | collective-permute-start | bytes 393224 | tf_op jit(solution)/shard_map/ppermute | solution.py:347
  4.8 0.8 %copy_bitcast_fusion = bf16[16,8,8,256]{3,2,1,0:T(8,128)(2,1)} fusion(bf16[8,128,256]{2,1,0:T(8,128)(2,1)S(1)} %copy-done), kind=kLoop, calls=%fused_computation.3 | loop fusion | bytes 1048576 | tf_op jit(solution)/shard_map/transpose | solution.py:384
  5.6 5.1 %all-to-all-start = ((bf16[16,8,8,256]{3,2,1,0:T(8,128)(2,1)}), bf16[16,8,8,256]{3,2,1,0:T(8,128)(2,1)S(1)}, u32[]{:S(2)}, u32[]{:S(2)}) async-start(bf16[16,8,8,256]{3,2,1,0:T(8,128)(2,1)} %copy_bitcast_fusion), calls=%async_computation | async-start | bytes 1048576 | tf_op jit(solution)/shard_map/all_to_all | solution.py:385
  10.7 0.0 copy-start.2
  10.8 0.1 reshape.147
  10.9 0.1 sub.44
  11.0 0.1 copy.37
  11.1 0.1 fusion.8
  11.2 0.1 convolution_divide_fusion
  11.3 0.2 convolution_divide_fusion.1
  11.5 0.1 clamp_add_fusion
  11.6 0.5 copy-done.8
  12.1 0.2 copy-done.7
  12.3 0.2 copy.39
  12.4 0.0 copy-start.5
  12.5 0.7 %copy-done.5 = bf16[65,128]{1,0:T(8,128)(2,1)S(1)} copy-done((bf16[65,128]{1,0:T(8,128)(2,1)S(1)}, bf16[65,128]{1,0:T(8,128)(2,1)}, u32[]{:S(2)}) %copy-start.5) | copy-done | bytes 16664
  13.2 0.3 convolution_add_fusion.base_ref
  13.4 0.0 copy-start.11
  13.4 0.4 copy-done.12
  13.9 0.3 copy-done.11
  14.2 0.1 copy.47
  14.3 0.1 reshape.151.share_ref
  14.4 0.1 reshape.152.share_ref
  14.4 0.6 copy-done.4
  15.0 0.1 copy.40
  15.1 0.0 copy-start.10
  15.1 0.7 %copy-done.10 = f32[256]{0:T(256)S(1)} copy-done((f32[256]{0:T(256)S(1)}, f32[256]{0:T(256)}, u32[]{:S(2)}) %copy-start.10) | copy-done | bytes 1048
  15.8 0.1 copy.42.intercept_ref
  16.0 0.1 copy.38
  16.2 0.3 convert_add_fusion.base_ref
  16.4 8.6 %all-to-all-done = bf16[16,8,8,256]{3,2,1,0:T(8,128)(2,1)S(1)} async-done(((bf16[16,8,8,256]{3,2,1,0:T(8,128)(2,1)}), bf16[16,8,8,256]{3,2,1,0:T(8,128)(2,1)S(1)}, u32[]{:S(2)}, u32[]{:S(2)}) %all-to-all-start) | async-done | bytes 524320 | tf_op jit(solution)/shard_map/all_to_all | solution.py:385
  25.0 4.2 %attention.1 = (bf16[1024,256]{1,0:T(8,128)(2,1)}, bf16[8,32,128]{2,1,0:T(8,128)(2,1)S(1)}, bf16[256,128]{1,0:T(8,128)(2,1)S(1)}) custom-call(bf16[1024,256]{1,0:T(8,128)(2,1)S(1)} %bitcast.42, bf16[128,128]{1,0:T(8,128)(2,1)S(1)} %pad.5.clone.bias_ref, f32[8,1,128]{2,1,0:T(1,128)S(1)} %bitcast.47, f32[2,256]{1,0:T(2,128)S(1)} %pad_maximum_fusion.3.gains_ref, ...), custom_call_target="tpu_custom_call" | custom-call | flops 805306368 | bytes 1048576 | tf_op jit(solution)/shard_map/attention/pallas_call | solution.py:169
  29.2 4.2 %all-to-all-start.1 = ((bf16[16,8,8,256]{3,2,1,0:T(8,128)(2,1)}), bf16[16,8,8,256]{3,2,1,0:T(8,128)(2,1)S(1)}, u32[]{:S(2)}, u32[]{:S(2)}) async-start(bf16[16,8,8,256]{3,2,1,0:T(8,128)(2,1)} %bitcast.22), calls=%async_computation.1 | async-start | bytes 1048576 | tf_op jit(solution)/shard_map/all_to_all | solution.py:463
  33.4 3.7 %collective-permute-start.3 = (bf16[1,256,128]{2,1,0:T(8,128)(2,1)S(1)}, bf16[1,256,128]{2,1,0:T(8,128)(2,1)S(1)}, u32[]{:S(2)}, u32[]{:S(2)}) collective-permute-start(bf16[1,256,128]{2,1,0:T(8,128)(2,1)S(1)} %bitcast.43), channel_id=1, source_target_pairs={{0,12},{1,13},{2,14},{3,15},{4,8},{5,9},{6,10},{7,11},{8,4},{9,5},... | collective-permute-start | bytes 196616 | tf_op jit(solution)/shard_map/ppermute | solution.py:347
  37.1 0.7 %collective-permute-start.1 = (bf16[1,256,128]{2,1,0:T(8,128)(2,1)S(1)}, bf16[1,256,128]{2,1,0:T(8,128)(2,1)S(1)}, u32[]{:S(2)}, u32[]{:S(2)}) collective-permute-start(bf16[1,256,128]{2,1,0:T(8,128)(2,1)S(1)} %bitcast.45), channel_id=1, source_target_pairs={{0,4},{1,5},{2,6},{3,7},{4,0},{5,1},{6,2},{7,3},{8,12},{9,13},{10,... | collective-permute-start | bytes 196616 | tf_op jit(solution)/shard_map/ppermute | solution.py:347
  37.8 10.9 %collective-permute-done.3 = bf16[1,256,128]{2,1,0:T(8,128)(2,1)S(1)} collective-permute-done((bf16[1,256,128]{2,1,0:T(8,128)(2,1)S(1)}, bf16[1,256,128]{2,1,0:T(8,128)(2,1)S(1)}, u32[]{:S(2)}, u32[]{:S(2)}) %collective-permute-start.3) | collective-permute-done | bytes 65568 | tf_op jit(solution)/shard_map/ppermute | solution.py:347
  48.7 5.5 %collective-permute-done.2 = bf16[1,256,128]{2,1,0:T(8,128)(2,1)S(1)} collective-permute-done((bf16[1,256,128]{2,1,0:T(8,128)(2,1)S(1)}, bf16[1,256,128]{2,1,0:T(8,128)(2,1)S(1)}, u32[]{:S(2)}, u32[]{:S(2)}) %collective-permute-start.2) | collective-permute-done | bytes 65568 | tf_op jit(solution)/shard_map/ppermute | solution.py:347
  54.3 0.1 collective-permute-start.4
  54.3 1.5 %collective-permute-start.5 = (bf16[8,32,128]{2,1,0:T(8,128)(2,1)S(1)}, bf16[8,32,128]{2,1,0:T(8,128)(2,1)S(1)}, u32[]{:S(2)}, u32[]{:S(2)}) collective-permute-start(bf16[8,32,128]{2,1,0:T(8,128)(2,1)S(1)} %get-tuple-element.15.left_ref), channel_id=1, source_target_pairs={{0,2},{1,3},{2,0},{3,1},{4,6},{5,7},{6,4},{7,5},{8,10},{9,11},{10,... | collective-permute-start | bytes 196616 | tf_op jit(solution)/shard_map/ppermute | solution.py:347
  55.9 0.1 copy.43.weight_ref
  56.0 2.8 %collective-permute-done.5.left_ref = bf16[8,32,128]{2,1,0:T(8,128)(2,1)S(1)} collective-permute-done((bf16[8,32,128]{2,1,0:T(8,128)(2,1)S(1)}, bf16[8,32,128]{2,1,0:T(8,128)(2,1)S(1)}, u32[]{:S(2)}, u32[]{:S(2)}) %collective-permute-start.5) | collective-permute-done | bytes 65568 | tf_op jit(solution)/shard_map/ppermute | solution.py:347
  58.8 1.3 %pair_part.3 = bf16[8,64,128]{2,1,0:T(8,128)(2,1)S(1)} custom-call(s32[1]{0:T(128)} %bitcast.me_ref, bf16[8,32,128]{2,1,0:T(8,128)(2,1)S(1)} %collective-permute-done.5.left_ref, bf16[128,1024]{1,0:T(8,128)(2,1)S(1)} %copy.43.weight_ref, f32[4,128]{1,0:T(4,128)S(1)} %reshape.152.share_ref, f32[8,64,128]{2,1,0:T(8,128)S(1)} %convert_add_fusion.base_ref, ...), custom_call_target="tpu_custom_call" | custom-call | flops 268435456 | bytes 524288 | tf_op jit(solution)/shard_map/pair_part/pallas_call | solution.py:272
  60.1 1.5 %collective-permute-start.6 = (bf16[8,64,128]{2,1,0:T(8,128)(2,1)S(1)}, bf16[8,64,128]{2,1,0:T(8,128)(2,1)S(1)}, u32[]{:S(2)}, u32[]{:S(2)}) collective-permute-start(bf16[8,64,128]{2,1,0:T(8,128)(2,1)S(1)} %pair_part.3), channel_id=1, source_target_pairs={{0,2},{1,3},{2,0},{3,1},{4,6},{5,7},{6,4},{7,5},{8,10},{9,11},{10,... | collective-permute-start | bytes 393224 | tf_op jit(solution)/shard_map/ppermute | solution.py:347
  61.6 1.3 %pair_part.2.refs_0_ = bf16[8,64,128]{2,1,0:T(8,128)(2,1)S(1)} custom-call(s32[1]{0:T(128)} %bitcast.me_ref, bf16[8,32,128]{2,1,0:T(8,128)(2,1)S(1)} %get-tuple-element.15.left_ref, bf16[128,1024]{1,0:T(8,128)(2,1)S(1)} %copy.43.weight_ref, f32[4,128]{1,0:T(4,128)S(1)} %reshape.151.share_ref, f32[8,64,128]{2,1,0:T(8,128)S(1)} %convolution_add_fusion.base_ref, ...), custom_call_target="tpu_custom_call" | custom-call | flops 268435456 | bytes 524288 | tf_op jit(solution)/shard_map/pair_part/pallas_call | solution.py:272
  62.9 2.2 %collective-permute-done.6.refs_1_ = bf16[8,64,128]{2,1,0:T(8,128)(2,1)S(1)} collective-permute-done((bf16[8,64,128]{2,1,0:T(8,128)(2,1)S(1)}, bf16[8,64,128]{2,1,0:T(8,128)(2,1)S(1)}, u32[]{:S(2)}, u32[]{:S(2)}) %collective-permute-start.6) | collective-permute-done | bytes 131104 | tf_op jit(solution)/shard_map/ppermute | solution.py:347
  65.2 1.0 %finish.1 = (bf16[8,128,128]{2,1,0:T(8,128)(2,1)}, bf16[8,16,8,256]{3,2,1,0:T(8,128)(2,1)}) custom-call(s32[1]{0:T(128)} %bitcast.me_ref, bf16[16,8,8,256]{3,2,1,0:T(8,128)(2,1)S(1)} %all-to-all-done.1.back_ref, bf16[8,64,128]{2,1,0:T(8,128)(2,1)S(1)} %pair_part.2.refs_0_, bf16[8,64,128]{2,1,0:T(8,128)(2,1)S(1)} %collective-permute-done.6.refs_1_), custom_call_target="tpu_custom_call" | custom-call | tf_op jit(solution)/shard_map/finish/pallas_call | solution.py:321
  (30 shorter events, 0.2 us)
Async XLA Ops:
  0.6 4.1 %copy-start = (bf16[8,128,256]{2,1,0:T(8,128)(2,1)S(1)}, bf16[8,128,256]{2,1,0:T(8,128)(2,1)}, u32[]{:S(2)}) copy-start(bf16[8,128,256]{2,1,0:T(8,128)(2,1)} %param.14) | copy-start | bytes 1572868
  1.7 14.4 %collective-permute-start = (bf16[8,64,128]{2,1,0:T(8,128)(2,1)S(1)}, bf16[8,64,128]{2,1,0:T(8,128)(2,1)S(1)}, u32[]{:S(2)}, u32[]{:S(2)}) collective-permute-start(bf16[8,64,128]{2,1,0:T(8,128)(2,1)S(1)} %bitcast.57), channel_id=1, source_target_pairs={{0,2},{1,3},{2,0},{3,1},{4,6},{5,7},{6,4},{7,5},{8,10},{9,11},{10,... | collective-permute-start | bytes 393224 | tf_op jit(solution)/shard_map/ppermute | solution.py:347
  5.6 5.1 %copy-start.9 = (s32[128]{0:T(128)S(1)}, s32[128]{0:T(128)}, u32[]{:S(2)}) copy-start(s32[128]{0:T(128)} %param.16) | copy-start | bytes 1540
  5.6 5.3 %copy-start.6 = (s32[128,128]{1,0:T(8,128)S(1)}, s32[128,128]{1,0:T(8,128)}, u32[]{:S(2)}) copy-start(s32[128,128]{1,0:T(8,128)} %param.15) | copy-start | bytes 196612
  5.6 19.4 %all-to-all-start = ((bf16[16,8,8,256]{3,2,1,0:T(8,128)(2,1)}), bf16[16,8,8,256]{3,2,1,0:T(8,128)(2,1)S(1)}, u32[]{:S(2)}, u32[]{:S(2)}) async-start(bf16[16,8,8,256]{3,2,1,0:T(8,128)(2,1)} %copy_bitcast_fusion), calls=%async_computation | async-start | bytes 1048576 | tf_op jit(solution)/shard_map/all_to_all | solution.py:385
  10.7 1.5 %copy-start.2 = (bf16[256,768]{1,0:T(8,128)(2,1)S(1)}, bf16[256,768]{1,0:T(8,128)(2,1)}, u32[]{:S(2)}) copy-start(bf16[256,768]{1,0:T(8,128)(2,1)} %param.19) | copy-start | bytes 1179652
  11.3 0.8 %copy-start.8 = (bf16[256,32]{0,1:T(8,128)(2,1)S(1)}, bf16[256,32]{0,1:T(8,128)(2,1)}, u32[]{:S(2)}) copy-start(bf16[256,32]{0,1:T(8,128)(2,1)} %param.24) | copy-start | bytes 49156
  11.5 0.8 %copy-start.7 = (bf16[256,32]{0,1:T(8,128)(2,1)S(1)}, bf16[256,32]{0,1:T(8,128)(2,1)}, u32[]{:S(2)}) copy-start(bf16[256,32]{0,1:T(8,128)(2,1)} %param.25) | copy-start | bytes 49156
  12.4 0.7 %copy-start.5 = (bf16[65,128]{1,0:T(8,128)(2,1)S(1)}, bf16[65,128]{1,0:T(8,128)(2,1)}, u32[]{:S(2)}) copy-start(bf16[65,128]{1,0:T(8,128)(2,1)} %param.27) | copy-start | bytes 49924
  13.2 0.7 %copy-start.12 = (f32[256]{0:T(256)S(1)}, f32[256]{0:T(256)}, u32[]{:S(2)}) copy-start(f32[256]{0:T(256)} %param.18) | copy-start | bytes 3076
  13.4 0.7 %copy-start.11 = (f32[256]{0:T(256)S(1)}, f32[256]{0:T(256)}, u32[]{:S(2)}) copy-start(f32[256]{0:T(256)} %param.23) | copy-start | bytes 3076
  14.1 0.9 %copy-start.4 = (bf16[256,256]{1,0:T(8,128)(2,1)S(1)}, bf16[256,256]{1,0:T(8,128)(2,1)}, u32[]{:S(2)}) copy-start(bf16[256,256]{1,0:T(8,128)(2,1)} %param.20) | copy-start | bytes 393220
  14.1 1.8 %copy-start.3 = (bf16[1024,128]{1,0:T(8,128)(2,1)S(1)}, bf16[1024,128]{1,0:T(8,128)(2,1)}, u32[]{:S(2)}) copy-start(bf16[1024,128]{1,0:T(8,128)(2,1)} %param.26) | copy-start | bytes 786436
  15.1 0.7 %copy-start.10 = (f32[256]{0:T(256)S(1)}, f32[256]{0:T(256)}, u32[]{:S(2)}) copy-start(f32[256]{0:T(256)} %param.21) | copy-start | bytes 3076
  16.1 8.9 %copy-start.1 = (bf16[256,256]{1,0:T(8,128)(2,1)S(1)}, bf16[256,256]{1,0:T(8,128)(2,1)}, u32[]{:S(2)}) copy-start(bf16[256,256]{1,0:T(8,128)(2,1)} %wo_ref.1) | copy-start | bytes 393220
  29.2 36.0 %all-to-all-start.1 = ((bf16[16,8,8,256]{3,2,1,0:T(8,128)(2,1)}), bf16[16,8,8,256]{3,2,1,0:T(8,128)(2,1)S(1)}, u32[]{:S(2)}, u32[]{:S(2)}) async-start(bf16[16,8,8,256]{3,2,1,0:T(8,128)(2,1)} %bitcast.22), calls=%async_computation.1 | async-start | bytes 1048576 | tf_op jit(solution)/shard_map/all_to_all | solution.py:463
  33.4 15.3 %collective-permute-start.3 = (bf16[1,256,128]{2,1,0:T(8,128)(2,1)S(1)}, bf16[1,256,128]{2,1,0:T(8,128)(2,1)S(1)}, u32[]{:S(2)}, u32[]{:S(2)}) collective-permute-start(bf16[1,256,128]{2,1,0:T(8,128)(2,1)S(1)} %bitcast.43), channel_id=1, source_target_pairs={{0,12},{1,13},{2,14},{3,15},{4,8},{5,9},{6,10},{7,11},{8,4},{9,5},... | collective-permute-start | bytes 196616 | tf_op jit(solution)/shard_map/ppermute | solution.py:347
  37.1 17.1 %collective-permute-start.2 = (bf16[1,256,128]{2,1,0:T(8,128)(2,1)S(1)}, bf16[1,256,128]{2,1,0:T(8,128)(2,1)S(1)}, u32[]{:S(2)}, u32[]{:S(2)}) collective-permute-start(bf16[1,256,128]{2,1,0:T(8,128)(2,1)S(1)} %bitcast.44), channel_id=1, source_target_pairs={{0,8},{1,9},{2,10},{3,11},{4,12},{5,13},{6,14},{7,15},{8,0},{9,1},... | collective-permute-start | bytes 196616 | tf_op jit(solution)/shard_map/ppermute | solution.py:347
  37.1 17.1 %collective-permute-start.1 = (bf16[1,256,128]{2,1,0:T(8,128)(2,1)S(1)}, bf16[1,256,128]{2,1,0:T(8,128)(2,1)S(1)}, u32[]{:S(2)}, u32[]{:S(2)}) collective-permute-start(bf16[1,256,128]{2,1,0:T(8,128)(2,1)S(1)} %bitcast.45), channel_id=1, source_target_pairs={{0,4},{1,5},{2,6},{3,7},{4,0},{5,1},{6,2},{7,3},{8,12},{9,13},{10,... | collective-permute-start | bytes 196616 | tf_op jit(solution)/shard_map/ppermute | solution.py:347
  54.3 4.6 %collective-permute-start.4 = (bf16[4,256,128]{2,1,0:T(8,128)(2,1)S(1)}, bf16[4,256,128]{2,1,0:T(8,128)(2,1)S(1)}, u32[]{:S(2)}, u32[]{:S(2)}) collective-permute-start(bf16[4,256,128]{2,1,0:T(8,128)(2,1)S(1)} %pad_maximum_fusion.1.refs_0_), channel_id=1, source_target_pairs={{0,1},{1,0},{2,3},{3,2},{4,5},{5,4},{6,7},{7,6},{8,9},{9,8},{10,11... | collective-permute-start | bytes 786440 | tf_op jit(solution)/shard_map/ppermute | solution.py:347
  54.3 4.5 %collective-permute-start.5 = (bf16[8,32,128]{2,1,0:T(8,128)(2,1)S(1)}, bf16[8,32,128]{2,1,0:T(8,128)(2,1)S(1)}, u32[]{:S(2)}, u32[]{:S(2)}) collective-permute-start(bf16[8,32,128]{2,1,0:T(8,128)(2,1)S(1)} %get-tuple-element.15.left_ref), channel_id=1, source_target_pairs={{0,2},{1,3},{2,0},{3,1},{4,6},{5,7},{6,4},{7,5},{8,10},{9,11},{10,... | collective-permute-start | bytes 196616 | tf_op jit(solution)/shard_map/ppermute | solution.py:347
  60.1 5.0 %collective-permute-start.6 = (bf16[8,64,128]{2,1,0:T(8,128)(2,1)S(1)}, bf16[8,64,128]{2,1,0:T(8,128)(2,1)S(1)}, u32[]{:S(2)}, u32[]{:S(2)}) collective-permute-start(bf16[8,64,128]{2,1,0:T(8,128)(2,1)S(1)} %pair_part.3), channel_id=1, source_target_pairs={{0,2},{1,3},{2,0},{3,1},{4,6},{5,7},{6,4},{7,5},{8,10},{9,11},{10,... | collective-permute-start | bytes 393224 | tf_op jit(solution)/shard_map/ppermute | solution.py:347

commit v4 on v2

--- a/solution.py
+++ b/solution.py
@@ -294,11 +294,14 @@
     part_refs, refs = refs[:near_size], refs[near_size:]
     pair_out_ref, changed_out_ref, pair_ref, changed_ref, sems = refs
     devices, sequences = back_ref.shape[:2]
-    for d in range(devices):
-        for n in range(sequences):
+    copies = []
+    for n in range(sequences):
+        for d in range(devices):
             changed_ref[n, d] = back_ref[d, n]
-    copies = [pltpu.make_async_copy(changed_ref, changed_out_ref, sems.at[0])]
-    copies[0].start()
+        copies.append(
+            pltpu.make_async_copy(changed_ref.at[n], changed_out_ref.at[n], sems.at[n])
+        )
+        copies[-1].start()
     chunk = part_refs[0].shape[1] // far_stage[1]
     near = digit(me_ref[0], near_stage)
     for n in range(near_size):
@@ -306,8 +309,8 @@
             chip = f * near_size + jnp.bitwise_xor(near, n)
             here = pl.ds(pl.multiple_of(chip * chunk, chunk), chunk)
             pair_ref[:, here, :] = part_refs[n][:, f * chunk : (f + 1) * chunk, :]
-    copies.append(pltpu.make_async_copy(pair_ref, pair_out_ref, sems.at[1]))
-    copies[1].start()
+    copies.append(pltpu.make_async_copy(pair_ref, pair_out_ref, sems.at[sequences]))
+    copies[-1].start()
     for copy in copies:
         copy.wait()
 
@@ -325,7 +328,7 @@
         scratch_shapes=[
             pltpu.VMEM(pair_shape, BF16),
             pltpu.VMEM(changed_shape, BF16),
-            pltpu.SemaphoreType.DMA((2,)),
+            pltpu.SemaphoreType.DMA((seq_local + 1,)),
         ],
         out_shape=(
             jax.ShapeDtypeStruct(pair_shape, BF16),

time: 66.7 us -> 66.7 us (level)
  no operation moved by 1% of the time
where the time goes in v4:
time: 66.7 us; the launch traced here: 66.2 us
  waiting for transfers between devices  30.1 us (45%)
  starting transfers between devices  19.9 us (30%)
  Pallas kernels  7.72 us (12%)
  local copies, waits for them, and re-layouts  6.55 us (10%)
  between operations  0.89 us (1%)
  matrix products  0.82 us (1%)
    ppermute x7, waiting for transfers between devices, exchange(): return lax.ppermute(held, 'wide', [(d, d ^ distance) for d in range(size)])  21.5 us
    ppermute x7, starting transfers between devices, exchange(): return lax.ppermute(held, 'wide', [(d, d ^ distance) for d in range(size)])  10.6 us
    all_to_all x1, waiting for transfers between devices, on_device(): x_rows = lax.all_to_all(sent, 'wide', 0, 0, tiled=True)  8.61 us
    all_to_all x1, starting transfers between devices, on_device(): x_rows = lax.all_to_all(sent, 'wide', 0, 0, tiled=True)  5.11 us
    pallas_call x1, Pallas kernels, attention(): pl.pallas_call(functools.partial(attention_kernel, tokens), out_shape=(ja...  4.22 us
    all_to_all x1, starting transfers between devices, on_device(): lax.all_to_all(changed_rows.reshape(size, seq_local, tok_local, channels)...  4.17 us
    unnamed x30, local copies, waits for them, and re-layouts  3.81 us
    pallas_call x2, Pallas kernels, pair_part(): pl.pallas_call(functools.partial(pair_kernel, stages), in_specs=[pl.Block...  2.53 us
  transfers between devices with their start and end apart: 9, of which 5 were waited for; matrix products, arithmetic and copies ran while one was open for 5% of the time, Pallas kernels for 4%

profile of v4, /device:TPU:0, one launch (start us, length us, event | category | flops | bytes accessed | tf_op | source)
XLA Modules:
  0.0 66.2 jit_solution(11617135241228732326)
XLA Ops:
  0.6 0.0 copy-start
  0.7 1.0 %constant_dynamic-slice_fusion.2 = (bf16[8,4,1,16,128]{4,3,2,1,0:T(8,128)(2,1)S(1)}, bf16[8,4,1,16,128]{4,3,2,1,0:T(8,128)(2,1)S(1)}) fusion(bf16[8,4,2,16,128]{4,3,2,1,0:T(8,128)(2,1)} %bitcast.54, s32[]{:T(128)S(6)} %select_n.28, s32[]{:T(128)S(6)} %select_n.26), kind=kLoop, calls=%fused_computation.24 | loop fusion | bytes 524296 | tf_op jit(solution)/shard_map/jit(dynamic_index_in_dim)/dynamic_slice | solution.py:417
  1.7 3.1 %collective-permute-start = (bf16[8,64,128]{2,1,0:T(8,128)(2,1)S(1)}, bf16[8,64,128]{2,1,0:T(8,128)(2,1)S(1)}, u32[]{:S(2)}, u32[]{:S(2)}) collective-permute-start(bf16[8,64,128]{2,1,0:T(8,128)(2,1)S(1)} %bitcast.57), channel_id=1, source_target_pairs={{0,2},{1,3},{2,0},{3,1},{4,6},{5,7},{6,4},{7,5},{8,10},{9,11},{10,... | collective-permute-start | bytes 393224 | tf_op jit(solution)/shard_map/ppermute | solution.py:350
  4.8 0.8 %copy_bitcast_fusion = bf16[16,8,8,256]{3,2,1,0:T(8,128)(2,1)} fusion(bf16[8,128,256]{2,1,0:T(8,128)(2,1)S(1)} %copy-done), kind=kLoop, calls=%fused_computation.3 | loop fusion | bytes 1048576 | tf_op jit(solution)/shard_map/transpose | solution.py:387
  5.6 5.1 %all-to-all-start = ((bf16[16,8,8,256]{3,2,1,0:T(8,128)(2,1)}), bf16[16,8,8,256]{3,2,1,0:T(8,128)(2,1)S(1)}, u32[]{:S(2)}, u32[]{:S(2)}) async-start(bf16[16,8,8,256]{3,2,1,0:T(8,128)(2,1)} %copy_bitcast_fusion), calls=%async_computation | async-start | bytes 1048576 | tf_op jit(solution)/shard_map/all_to_all | solution.py:388
  10.7 0.0 copy-start.2
  10.8 0.1 reshape.147
  10.9 0.1 sub.44
  11.0 0.1 copy.37
  11.1 0.1 fusion.8
  11.2 0.1 convolution_divide_fusion
  11.3 0.2 convolution_divide_fusion.1
  11.5 0.1 clamp_add_fusion
  11.6 0.5 copy-done.8
  12.1 0.2 copy-done.7
  12.3 0.2 copy.39
  12.4 0.0 copy-start.5
  12.5 0.7 %copy-done.5 = bf16[65,128]{1,0:T(8,128)(2,1)S(1)} copy-done((bf16[65,128]{1,0:T(8,128)(2,1)S(1)}, bf16[65,128]{1,0:T(8,128)(2,1)}, u32[]{:S(2)}) %copy-start.5) | copy-done | bytes 16664
  13.2 0.3 convolution_add_fusion.base_ref
  13.4 0.0 copy-start.11
  13.4 0.4 copy-done.12
  13.9 0.3 copy-done.11
  14.2 0.1 copy.47
  14.3 0.1 reshape.151.share_ref
  14.4 0.1 reshape.152.share_ref
  14.4 0.6 copy-done.4
  15.0 0.1 copy.40
  15.1 0.0 copy-start.10
  15.1 0.7 %copy-done.10 = f32[256]{0:T(256)S(1)} copy-done((f32[256]{0:T(256)S(1)}, f32[256]{0:T(256)}, u32[]{:S(2)}) %copy-start.10) | copy-done | bytes 1048
  15.8 0.1 copy.42.intercept_ref
  16.0 0.1 copy.38
  16.2 0.3 convert_add_fusion.base_ref
  16.4 8.6 %all-to-all-done = bf16[16,8,8,256]{3,2,1,0:T(8,128)(2,1)S(1)} async-done(((bf16[16,8,8,256]{3,2,1,0:T(8,128)(2,1)}), bf16[16,8,8,256]{3,2,1,0:T(8,128)(2,1)S(1)}, u32[]{:S(2)}, u32[]{:S(2)}) %all-to-all-start) | async-done | bytes 524320 | tf_op jit(solution)/shard_map/all_to_all | solution.py:388
  25.0 4.2 %attention.1 = (bf16[1024,256]{1,0:T(8,128)(2,1)}, bf16[8,32,128]{2,1,0:T(8,128)(2,1)S(1)}, bf16[256,128]{1,0:T(8,128)(2,1)S(1)}) custom-call(bf16[1024,256]{1,0:T(8,128)(2,1)S(1)} %bitcast.42, bf16[128,128]{1,0:T(8,128)(2,1)S(1)} %pad.5.clone.bias_ref, f32[8,1,128]{2,1,0:T(1,128)S(1)} %bitcast.47, f32[2,256]{1,0:T(2,128)S(1)} %pad_maximum_fusion.3.gains_ref, ...), custom_call_target="tpu_custom_call" | custom-call | flops 805306368 | bytes 1048576 | tf_op jit(solution)/shard_map/attention/pallas_call | solution.py:169
  29.2 4.2 %all-to-all-start.1 = ((bf16[16,8,8,256]{3,2,1,0:T(8,128)(2,1)}), bf16[16,8,8,256]{3,2,1,0:T(8,128)(2,1)S(1)}, u32[]{:S(2)}, u32[]{:S(2)}) async-start(bf16[16,8,8,256]{3,2,1,0:T(8,128)(2,1)} %bitcast.22), calls=%async_computation.1 | async-start | bytes 1048576 | tf_op jit(solution)/shard_map/all_to_all | solution.py:466
  33.4 3.7 %collective-permute-start.3 = (bf16[1,256,128]{2,1,0:T(8,128)(2,1)S(1)}, bf16[1,256,128]{2,1,0:T(8,128)(2,1)S(1)}, u32[]{:S(2)}, u32[]{:S(2)}) collective-permute-start(bf16[1,256,128]{2,1,0:T(8,128)(2,1)S(1)} %bitcast.43), channel_id=1, source_target_pairs={{0,12},{1,13},{2,14},{3,15},{4,8},{5,9},{6,10},{7,11},{8,4},{9,5},... | collective-permute-start | bytes 196616 | tf_op jit(solution)/shard_map/ppermute | solution.py:350
  37.2 0.7 %collective-permute-start.1 = (bf16[1,256,128]{2,1,0:T(8,128)(2,1)S(1)}, bf16[1,256,128]{2,1,0:T(8,128)(2,1)S(1)}, u32[]{:S(2)}, u32[]{:S(2)}) collective-permute-start(bf16[1,256,128]{2,1,0:T(8,128)(2,1)S(1)} %bitcast.45), channel_id=1, source_target_pairs={{0,4},{1,5},{2,6},{3,7},{4,0},{5,1},{6,2},{7,3},{8,12},{9,13},{10,... | collective-permute-start | bytes 196616 | tf_op jit(solution)/shard_map/ppermute | solution.py:350
  37.9 10.9 %collective-permute-done.3 = bf16[1,256,128]{2,1,0:T(8,128)(2,1)S(1)} collective-permute-done((bf16[1,256,128]{2,1,0:T(8,128)(2,1)S(1)}, bf16[1,256,128]{2,1,0:T(8,128)(2,1)S(1)}, u32[]{:S(2)}, u32[]{:S(2)}) %collective-permute-start.3) | collective-permute-done | bytes 65568 | tf_op jit(solution)/shard_map/ppermute | solution.py:350
  48.8 5.5 %collective-permute-done.2 = bf16[1,256,128]{2,1,0:T(8,128)(2,1)S(1)} collective-permute-done((bf16[1,256,128]{2,1,0:T(8,128)(2,1)S(1)}, bf16[1,256,128]{2,1,0:T(8,128)(2,1)S(1)}, u32[]{:S(2)}, u32[]{:S(2)}) %collective-permute-start.2) | collective-permute-done | bytes 65568 | tf_op jit(solution)/shard_map/ppermute | solution.py:350
  54.3 0.1 collective-permute-start.4
  54.4 1.5 %collective-permute-start.5 = (bf16[8,32,128]{2,1,0:T(8,128)(2,1)S(1)}, bf16[8,32,128]{2,1,0:T(8,128)(2,1)S(1)}, u32[]{:S(2)}, u32[]{:S(2)}) collective-permute-start(bf16[8,32,128]{2,1,0:T(8,128)(2,1)S(1)} %get-tuple-element.15.left_ref), channel_id=1, source_target_pairs={{0,2},{1,3},{2,0},{3,1},{4,6},{5,7},{6,4},{7,5},{8,10},{9,11},{10,... | collective-permute-start | bytes 196616 | tf_op jit(solution)/shard_map/ppermute | solution.py:350
  55.9 0.1 copy.43.weight_ref
  56.1 2.8 %collective-permute-done.5.left_ref = bf16[8,32,128]{2,1,0:T(8,128)(2,1)S(1)} collective-permute-done((bf16[8,32,128]{2,1,0:T(8,128)(2,1)S(1)}, bf16[8,32,128]{2,1,0:T(8,128)(2,1)S(1)}, u32[]{:S(2)}, u32[]{:S(2)}) %collective-permute-start.5) | collective-permute-done | bytes 65568 | tf_op jit(solution)/shard_map/ppermute | solution.py:350
  58.9 1.3 %pair_part.3 = bf16[8,64,128]{2,1,0:T(8,128)(2,1)S(1)} custom-call(s32[1]{0:T(128)} %bitcast.me_ref, bf16[8,32,128]{2,1,0:T(8,128)(2,1)S(1)} %collective-permute-done.5.left_ref, bf16[128,1024]{1,0:T(8,128)(2,1)S(1)} %copy.43.weight_ref, f32[4,128]{1,0:T(4,128)S(1)} %reshape.152.share_ref, f32[8,64,128]{2,1,0:T(8,128)S(1)} %convert_add_fusion.base_ref, ...), custom_call_target="tpu_custom_call" | custom-call | flops 268435456 | bytes 524288 | tf_op jit(solution)/shard_map/pair_part/pallas_call | solution.py:272
  60.2 1.5 %collective-permute-start.6 = (bf16[8,64,128]{2,1,0:T(8,128)(2,1)S(1)}, bf16[8,64,128]{2,1,0:T(8,128)(2,1)S(1)}, u32[]{:S(2)}, u32[]{:S(2)}) collective-permute-start(bf16[8,64,128]{2,1,0:T(8,128)(2,1)S(1)} %pair_part.3), channel_id=1, source_target_pairs={{0,2},{1,3},{2,0},{3,1},{4,6},{5,7},{6,4},{7,5},{8,10},{9,11},{10,... | collective-permute-start | bytes 393224 | tf_op jit(solution)/shard_map/ppermute | solution.py:350
  61.7 1.3 %pair_part.2.refs_0_ = bf16[8,64,128]{2,1,0:T(8,128)(2,1)S(1)} custom-call(s32[1]{0:T(128)} %bitcast.me_ref, bf16[8,32,128]{2,1,0:T(8,128)(2,1)S(1)} %get-tuple-element.15.left_ref, bf16[128,1024]{1,0:T(8,128)(2,1)S(1)} %copy.43.weight_ref, f32[4,128]{1,0:T(4,128)S(1)} %reshape.151.share_ref, f32[8,64,128]{2,1,0:T(8,128)S(1)} %convolution_add_fusion.base_ref, ...), custom_call_target="tpu_custom_call" | custom-call | flops 268435456 | bytes 524288 | tf_op jit(solution)/shard_map/pair_part/pallas_call | solution.py:272
  63.0 2.2 %collective-permute-done.6.refs_1_ = bf16[8,64,128]{2,1,0:T(8,128)(2,1)S(1)} collective-permute-done((bf16[8,64,128]{2,1,0:T(8,128)(2,1)S(1)}, bf16[8,64,128]{2,1,0:T(8,128)(2,1)S(1)}, u32[]{:S(2)}, u32[]{:S(2)}) %collective-permute-start.6) | collective-permute-done | bytes 131104 | tf_op jit(solution)/shard_map/ppermute | solution.py:350
  65.2 1.0 %finish.1 = (bf16[8,128,128]{2,1,0:T(8,128)(2,1)}, bf16[8,16,8,256]{3,2,1,0:T(8,128)(2,1)}) custom-call(s32[1]{0:T(128)} %bitcast.me_ref, bf16[16,8,8,256]{3,2,1,0:T(8,128)(2,1)S(1)} %all-to-all-done.1.back_ref, bf16[8,64,128]{2,1,0:T(8,128)(2,1)S(1)} %pair_part.2.refs_0_, bf16[8,64,128]{2,1,0:T(8,128)(2,1)S(1)} %collective-permute-done.6.refs_1_), custom_call_target="tpu_custom_call" | custom-call | tf_op jit(solution)/shard_map/finish/pallas_call | solution.py:324
  (30 shorter events, 0.2 us)
Async XLA Ops:
  0.6 4.1 %copy-start = (bf16[8,128,256]{2,1,0:T(8,128)(2,1)S(1)}, bf16[8,128,256]{2,1,0:T(8,128)(2,1)}, u32[]{:S(2)}) copy-start(bf16[8,128,256]{2,1,0:T(8,128)(2,1)} %param.14) | copy-start | bytes 1572868
  1.7 14.4 %collective-permute-start = (bf16[8,64,128]{2,1,0:T(8,128)(2,1)S(1)}, bf16[8,64,128]{2,1,0:T(8,128)(2,1)S(1)}, u32[]{:S(2)}, u32[]{:S(2)}) collective-permute-start(bf16[8,64,128]{2,1,0:T(8,128)(2,1)S(1)} %bitcast.57), channel_id=1, source_target_pairs={{0,2},{1,3},{2,0},{3,1},{4,6},{5,7},{6,4},{7,5},{8,10},{9,11},{10,... | collective-permute-start | bytes 393224 | tf_op jit(solution)/shard_map/ppermute | solution.py:350
  5.6 5.1 %copy-start.9 = (s32[128]{0:T(128)S(1)}, s32[128]{0:T(128)}, u32[]{:S(2)}) copy-start(s32[128]{0:T(128)} %param.16) | copy-start | bytes 1540
  5.6 5.3 %copy-start.6 = (s32[128,128]{1,0:T(8,128)S(1)}, s32[128,128]{1,0:T(8,128)}, u32[]{:S(2)}) copy-start(s32[128,128]{1,0:T(8,128)} %param.15) | copy-start | bytes 196612
  5.6 19.4 %all-to-all-start = ((bf16[16,8,8,256]{3,2,1,0:T(8,128)(2,1)}), bf16[16,8,8,256]{3,2,1,0:T(8,128)(2,1)S(1)}, u32[]{:S(2)}, u32[]{:S(2)}) async-start(bf16[16,8,8,256]{3,2,1,0:T(8,128)(2,1)} %copy_bitcast_fusion), calls=%async_computation | async-start | bytes 1048576 | tf_op jit(solution)/shard_map/all_to_all | solution.py:388
  10.7 1.5 %copy-start.2 = (bf16[256,768]{1,0:T(8,128)(2,1)S(1)}, bf16[256,768]{1,0:T(8,128)(2,1)}, u32[]{:S(2)}) copy-start(bf16[256,768]{1,0:T(8,128)(2,1)} %param.19) | copy-start | bytes 1179652
  11.3 0.8 %copy-start.8 = (bf16[256,32]{0,1:T(8,128)(2,1)S(1)}, bf16[256,32]{0,1:T(8,128)(2,1)}, u32[]{:S(2)}) copy-start(bf16[256,32]{0,1:T(8,128)(2,1)} %param.24) | copy-start | bytes 49156
  11.5 0.8 %copy-start.7 = (bf16[256,32]{0,1:T(8,128)(2,1)S(1)}, bf16[256,32]{0,1:T(8,128)(2,1)}, u32[]{:S(2)}) copy-start(bf16[256,32]{0,1:T(8,128)(2,1)} %param.25) | copy-start | bytes 49156
  12.4 0.7 %copy-start.5 = (bf16[65,128]{1,0:T(8,128)(2,1)S(1)}, bf16[65,128]{1,0:T(8,128)(2,1)}, u32[]{:S(2)}) copy-start(bf16[65,128]{1,0:T(8,128)(2,1)} %param.27) | copy-start | bytes 49924
  13.2 0.7 %copy-start.12 = (f32[256]{0:T(256)S(1)}, f32[256]{0:T(256)}, u32[]{:S(2)}) copy-start(f32[256]{0:T(256)} %param.18) | copy-start | bytes 3076
  13.4 0.7 %copy-start.11 = (f32[256]{0:T(256)S(1)}, f32[256]{0:T(256)}, u32[]{:S(2)}) copy-start(f32[256]{0:T(256)} %param.23) | copy-start | bytes 3076
  14.1 0.9 %copy-start.4 = (bf16[256,256]{1,0:T(8,128)(2,1)S(1)}, bf16[256,256]{1,0:T(8,128)(2,1)}, u32[]{:S(2)}) copy-start(bf16[256,256]{1,0:T(8,128)(2,1)} %param.20) | copy-start | bytes 393220
  14.1 1.8 %copy-start.3 = (bf16[1024,128]{1,0:T(8,128)(2,1)S(1)}, bf16[1024,128]{1,0:T(8,128)(2,1)}, u32[]{:S(2)}) copy-start(bf16[1024,128]{1,0:T(8,128)(2,1)} %param.26) | copy-start | bytes 786436
  15.1 0.7 %copy-start.10 = (f32[256]{0:T(256)S(1)}, f32[256]{0:T(256)}, u32[]{:S(2)}) copy-start(f32[256]{0:T(256)} %param.21) | copy-start | bytes 3076
  16.1 8.9 %copy-start.1 = (bf16[256,256]{1,0:T(8,128)(2,1)S(1)}, bf16[256,256]{1,0:T(8,128)(2,1)}, u32[]{:S(2)}) copy-start(bf16[256,256]{1,0:T(8,128)(2,1)} %wo_ref.1) | copy-start | bytes 393220
  29.2 36.0 %all-to-all-start.1 = ((bf16[16,8,8,256]{3,2,1,0:T(8,128)(2,1)}), bf16[16,8,8,256]{3,2,1,0:T(8,128)(2,1)S(1)}, u32[]{:S(2)}, u32[]{:S(2)}) async-start(bf16[16,8,8,256]{3,2,1,0:T(8,128)(2,1)} %bitcast.22), calls=%async_computation.1 | async-start | bytes 1048576 | tf_op jit(solution)/shard_map/all_to_all | solution.py:466
  33.4 15.3 %collective-permute-start.3 = (bf16[1,256,128]{2,1,0:T(8,128)(2,1)S(1)}, bf16[1,256,128]{2,1,0:T(8,128)(2,1)S(1)}, u32[]{:S(2)}, u32[]{:S(2)}) collective-permute-start(bf16[1,256,128]{2,1,0:T(8,128)(2,1)S(1)} %bitcast.43), channel_id=1, source_target_pairs={{0,12},{1,13},{2,14},{3,15},{4,8},{5,9},{6,10},{7,11},{8,4},{9,5},... | collective-permute-start | bytes 196616 | tf_op jit(solution)/shard_map/ppermute | solution.py:350
  37.2 17.1 %collective-permute-start.2 = (bf16[1,256,128]{2,1,0:T(8,128)(2,1)S(1)}, bf16[1,256,128]{2,1,0:T(8,128)(2,1)S(1)}, u32[]{:S(2)}, u32[]{:S(2)}) collective-permute-start(bf16[1,256,128]{2,1,0:T(8,128)(2,1)S(1)} %bitcast.44), channel_id=1, source_target_pairs={{0,8},{1,9},{2,10},{3,11},{4,12},{5,13},{6,14},{7,15},{8,0},{9,1},... | collective-permute-start | bytes 196616 | tf_op jit(solution)/shard_map/ppermute | solution.py:350
  37.2 17.1 %collective-permute-start.1 = (bf16[1,256,128]{2,1,0:T(8,128)(2,1)S(1)}, bf16[1,256,128]{2,1,0:T(8,128)(2,1)S(1)}, u32[]{:S(2)}, u32[]{:S(2)}) collective-permute-start(bf16[1,256,128]{2,1,0:T(8,128)(2,1)S(1)} %bitcast.45), channel_id=1, source_target_pairs={{0,4},{1,5},{2,6},{3,7},{4,0},{5,1},{6,2},{7,3},{8,12},{9,13},{10,... | collective-permute-start | bytes 196616 | tf_op jit(solution)/shard_map/ppermute | solution.py:350
  54.3 4.6 %collective-permute-start.4 = (bf16[4,256,128]{2,1,0:T(8,128)(2,1)S(1)}, bf16[4,256,128]{2,1,0:T(8,128)(2,1)S(1)}, u32[]{:S(2)}, u32[]{:S(2)}) collective-permute-start(bf16[4,256,128]{2,1,0:T(8,128)(2,1)S(1)} %pad_maximum_fusion.1.refs_0_), channel_id=1, source_target_pairs={{0,1},{1,0},{2,3},{3,2},{4,5},{5,4},{6,7},{7,6},{8,9},{9,8},{10,11... | collective-permute-start | bytes 786440 | tf_op jit(solution)/shard_map/ppermute | solution.py:350
  54.4 4.5 %collective-permute-start.5 = (bf16[8,32,128]{2,1,0:T(8,128)(2,1)S(1)}, bf16[8,32,128]{2,1,0:T(8,128)(2,1)S(1)}, u32[]{:S(2)}, u32[]{:S(2)}) collective-permute-start(bf16[8,32,128]{2,1,0:T(8,128)(2,1)S(1)} %get-tuple-element.15.left_ref), channel_id=1, source_target_pairs={{0,2},{1,3},{2,0},{3,1},{4,6},{5,7},{6,4},{7,5},{8,10},{9,11},{10,... | collective-permute-start | bytes 196616 | tf_op jit(solution)/shard_map/ppermute | solution.py:350
  60.2 5.0 %collective-permute-start.6 = (bf16[8,64,128]{2,1,0:T(8,128)(2,1)S(1)}, bf16[8,64,128]{2,1,0:T(8,128)(2,1)S(1)}, u32[]{:S(2)}, u32[]{:S(2)}) collective-permute-start(bf16[8,64,128]{2,1,0:T(8,128)(2,1)S(1)} %pair_part.3), channel_id=1, source_target_pairs={{0,2},{1,3},{2,0},{3,1},{4,6},{5,7},{6,4},{7,5},{8,10},{9,11},{10,... | collective-permute-start | bytes 393224 | tf_op jit(solution)/shard_map/ppermute | solution.py:350
